TPU v7x, 256 devices: a whole 4x4x8 slice. The times are simulated.
256 devices in a mesh: feat: 16 (over z_lo, y), tok: 16 (over z_hi, x, core).
Axes of the slice: x: 4, y: 4, z: 8 (z_hi: 2, z_lo: 4; z = z_hi * 4 + z_lo), core: 2. Of those that a mesh axis runs over, the one named last changes fastest.
Arguments:
- tokens: bfloat16 [16384, 16384], P('tok', 'feat'), parts along dimension 0, may hold values from -6 to 6
- pair_weights: bfloat16 [2, 2048, 16384], P(None, None, 'feat'), may hold values from -0.125 to 0.125
- rank_down: bfloat16 [16384, 256], P('feat'), may hold values from -0.046875 to 0.046875
- rank_up: bfloat16 [256, 16384], P(None, 'feat'), may hold values from -0.375 to 0.375
Outputs:
- mixed: bfloat16 [16384, 16384], P('tok', 'feat'), parts along dimension 0
There are 16 independent parts, one for each index of `tok`. A program takes and returns all parts, laid end to end along the dimension named above; an argument that names none is the same for every part. Nothing has to cross between parts.
All inputs are finite; a program needn't handle non-finite values.
Results may differ from a plain program's by a relative error of at most 0.0049.
Values may be sent and summed in bfloat16 or wider, within the bound.
No kernel may reach another device: no remote copies, remote signals or barrier semaphores. Data moves between devices by JAX's collectives and lax.ppermute only.
A program may use at most 64 MiB of HBM per device.

v0:
```python
import jax
import jax.numpy as jnp
from jax import lax
from jax.sharding import PartitionSpec as P


def padded_to(lines, devices):
    spare = -len(lines) % devices
    return jnp.pad(lines, [(0, spare)] + [(0, 0)] * (lines.ndim - 1))


def sum_by_parts(value, axis):
    lines = value.reshape(-1, *value.shape[1:][-1:])
    padded = padded_to(lines, lax.axis_size(axis))
    own = lax.psum_scatter(padded, axis, scatter_dimension=0, tiled=True)
    whole = lax.all_gather(own, axis, axis=0, tiled=True)
    return whole[: len(lines)].reshape(value.shape)


def swapped(block, axis, stride):
    count = lax.axis_size(axis)
    route = []
    for low in range(count):
        high = low | 1 << stride
        if high != low and high < count:
            route += [(low, high), (high, low)]
    return lax.ppermute(block, axis, route)


def pair_product(own_rows, partner_rows, section_weight):
    block_width = own_rows.shape[1]
    first = jnp.dot(own_rows, section_weight[:block_width], preferred_element_type=jnp.float32)
    second = jnp.dot(partner_rows, section_weight[block_width:], preferred_element_type=jnp.float32)
    return first + second


def on_device(tokens, pair_weights, rank_down, rank_up):
    bit_levels = lax.axis_size("feat").bit_length() - 1
    section_count = pair_weights.shape[0]
    current = tokens
    activated = None
    for section_index in range(section_count):
        bit_number = section_index * (bit_levels - 1) // (section_count - 1)
        section_weight = pair_weights[section_index]
        half_rows = current.shape[0] // 2
        half_parts = []
        for half_index in range(2):
            own_rows = current[half_index * half_rows : (half_index + 1) * half_rows]
            partner_rows = swapped(own_rows, "feat", bit_number)
            half_parts.append(pair_product(own_rows, partner_rows, section_weight))
        pre_act = jnp.concatenate(half_parts, 0)
        activated = jax.nn.silu(pre_act)
        current = activated.astype(jnp.bfloat16)
    partial_value = jnp.dot(tokens, rank_down, preferred_element_type=jnp.float32)
    rank_total = sum_by_parts(partial_value, "feat")
    branch_out = jnp.dot(
        rank_total.astype(jnp.bfloat16), rank_up, preferred_element_type=jnp.float32
    )
    return (activated + branch_out).astype(jnp.bfloat16)


def solution(mesh):
    return jax.shard_map(
        on_device,
        mesh=mesh,
        in_specs=(P("tok", "feat"), P(None, None, "feat"), P("feat", None), P(None, "feat")),
        out_specs=P("tok", "feat"),
        check_vma=False,
    )
```

profile of v0, /device:TPU:1, one launch (start us, length us, event | category | flops | bytes accessed | tf_op | source)
XLA Modules:
  0.0 205.5 jit_solution(12205908195557919438)
XLA Ops:
  6.5 0.0 copy-start
  6.5 0.0 copy-start.1
  6.5 0.0 copy-start.2
  6.5 0.0 reduce-scatter.2.cloned.1.call-start
  6.5 3.2 %fusion.42 = (bf16[512,1024]{1,0:T(8,128)(2,1)}, bf16[512,1024]{1,0:T(8,128)(2,1)}) fusion(bf16[1024,1024]{1,0:T(8,128)(2,1)} %param.4), kind=kLoop, calls=%fused_computation.38 | loop fusion | bytes 4194304 | tf_op jit(solution)/shard_map/slice | solution.py:48
  9.7 2.1 %collective-permute-start = (bf16[512,1024]{1,0:T(8,128)(2,1)}, bf16[512,1024]{1,0:T(8,128)(2,1)}, u32[]{:S(2)}, u32[]{:S(2)}) collective-permute-start(bf16[512,1024]{1,0:T(8,128)(2,1)} %get-tuple-element.7), channel_id=1, source_target_pairs={{0,16},{16,0},{32,48},{48,32},{64,80},{80,64},{96,112},{112,96},{1... | collective-permute-start | bytes 3145736 | tf_op jit(solution)/shard_map/ppermute | solution.py:27
  11.8 0.0 collective-permute-start.1
  11.9 0.0 copy-done.1
  11.9 0.0 copy-done.2
  11.9 1.7 fusion.43
  13.5 0.0 reduce-scatter.2.cloned.1.call-update
  13.6 0.0 all-gather.2.cloned.1.call-start
  13.6 2.8 %fusion.14 = f32[512,1024]{1,0:T(8,128)S(1)} fusion(bf16[2,2048,1024]{2,1,0:T(8,128)(2,1)} %param.5, bf16[1024,1024]{1,0:T(8,128)(2,1)S(1)} %copy-done.1), kind=kOutput, calls=%fused_computation.18 | convolution fusion | flops 1073741824 | bytes 5242880 | tf_op jit(solution)/shard_map/dot_general | solution.py:32
  16.5 2.8 %fusion.12 = f32[512,1024]{1,0:T(8,128)S(1)} fusion(bf16[2,2048,1024]{2,1,0:T(8,128)(2,1)} %param.5, bf16[1024,1024]{1,0:T(8,128)(2,1)S(1)} %copy-done.1), kind=kOutput, calls=%fused_computation.16 | convolution fusion | flops 1073741824 | bytes 5242880 | tf_op jit(solution)/shard_map/dot_general | solution.py:32
  19.3 15.3 %collective-permute-done = bf16[512,1024]{1,0:T(8,128)(2,1)} collective-permute-done((bf16[512,1024]{1,0:T(8,128)(2,1)}, bf16[512,1024]{1,0:T(8,128)(2,1)}, u32[]{:S(2)}, u32[]{:S(2)}) %collective-permute-start) | collective-permute-done | bytes 1048608 | tf_op jit(solution)/shard_map/ppermute | solution.py:27
  34.6 3.2 %fusion.24 = f32[512,1024]{1,0:T(8,128)S(1)} fusion(f32[512,1024]{1,0:T(8,128)S(1)} %fusion.14, bf16[512,1024]{1,0:T(8,128)(2,1)} %collective-permute-done, bf16[2,2048,1024]{2,1,0:T(8,128)(2,1)} %param.5), kind=kOutput, calls=%fused_computation.28 | convolution fusion | flops 1074266112 | bytes 7340032 | tf_op jit(solution)/shard_map/dot_general | solution.py:33
  37.8 23.8 %collective-permute-done.1 = bf16[512,1024]{1,0:T(8,128)(2,1)} collective-permute-done((bf16[512,1024]{1,0:T(8,128)(2,1)}, bf16[512,1024]{1,0:T(8,128)(2,1)}, u32[]{:S(2)}, u32[]{:S(2)}) %collective-permute-start.1) | collective-permute-done | bytes 1048608 | tf_op jit(solution)/shard_map/ppermute | solution.py:27
  61.6 3.2 %fusion.27 = f32[512,1024]{1,0:T(8,128)S(1)} fusion(f32[512,1024]{1,0:T(8,128)S(1)} %fusion.12, bf16[512,1024]{1,0:T(8,128)(2,1)} %collective-permute-done.1, bf16[2,2048,1024]{2,1,0:T(8,128)(2,1)} %param.5), kind=kOutput, calls=%fused_computation.29 | convolution fusion | flops 1074266112 | bytes 7340032 | tf_op jit(solution)/shard_map/dot_general | solution.py:33
  64.8 1.2 multiply_convert_fusion
  66.0 27.0 %reduce-scatter.2.cloned.1.call-done = f32[64,256]{1,0:T(8,128)} async-done(((f32[1024,256]{1,0:T(8,128)}), f32[64,256]{1,0:T(8,128)}) %reduce-scatter.2.cloned.1.call-update) | async-done | bytes 65552 | tf_op jit(solution)/shard_map/reduce_scatter | solution.py:15
  92.9 0.0 all-gather.2.cloned.1.call-update
  93.0 0.2 fusion.41
  93.2 0.1 collective-permute-start.2
  93.3 2.4 %collective-permute-start.3 = (bf16[512,1024]{1,0:T(8,128)(2,1)S(1)}, bf16[512,1024]{1,0:T(8,128)(2,1)S(1)}, u32[]{:S(2)}, u32[]{:S(2)}) collective-permute-start(bf16[512,1024]{1,0:T(8,128)(2,1)S(1)} %get-tuple-element.6), channel_id=1, source_target_pairs={{0,128},{128,0},{16,144},{144,16},{32,160},{160,32},{48,176},{176,... | collective-permute-start | bytes 3145736 | tf_op jit(solution)/shard_map/ppermute | solution.py:27
  95.6 0.0 slice-start
  95.6 3.0 %fusion.6 = f32[512,1024]{1,0:T(8,128)S(1)} fusion(bf16[2,2048,1024]{2,1,0:T(8,128)(2,1)} %param.5, bf16[1024,1024]{1,0:T(8,128)(2,1)S(1)} %multiply_convert_fusion), kind=kOutput, calls=%fused_computation.10 | convolution fusion | flops 1073741824 | bytes 5242880 | tf_op jit(solution)/shard_map/dot_general | solution.py:32
  98.6 0.0 slice-start.1
  98.6 3.0 %fusion.4 = f32[512,1024]{1,0:T(8,128)S(1)} fusion(bf16[2,2048,1024]{2,1,0:T(8,128)(2,1)} %param.5, bf16[1024,1024]{1,0:T(8,128)(2,1)S(1)} %multiply_convert_fusion), kind=kOutput, calls=%fused_computation.8 | convolution fusion | flops 1073741824 | bytes 5242880 | tf_op jit(solution)/shard_map/dot_general | solution.py:32
  101.6 64.8 %collective-permute-done.2 = bf16[512,1024]{1,0:T(8,128)(2,1)S(1)} collective-permute-done((bf16[512,1024]{1,0:T(8,128)(2,1)S(1)}, bf16[512,1024]{1,0:T(8,128)(2,1)S(1)}, u32[]{:S(2)}, u32[]{:S(2)}) %collective-permute-start.2) | collective-permute-done | bytes 1048608 | tf_op jit(solution)/shard_map/ppermute | solution.py:27
  166.4 0.0 slice-done
  166.4 0.0 slice-done.1
  166.4 1.3 fusion.30
  167.7 23.9 %collective-permute-done.3 = bf16[512,1024]{1,0:T(8,128)(2,1)S(1)} collective-permute-done((bf16[512,1024]{1,0:T(8,128)(2,1)S(1)}, bf16[512,1024]{1,0:T(8,128)(2,1)S(1)}, u32[]{:S(2)}, u32[]{:S(2)}) %collective-permute-start.3) | collective-permute-done | bytes 1048608 | tf_op jit(solution)/shard_map/ppermute | solution.py:27
  191.6 2.6 %fusion.33 = f32[512,1024]{1,0:T(8,128)} fusion(f32[512,1024]{1,0:T(8,128)S(1)} %fusion.4, bf16[512,1024]{1,0:T(8,128)(2,1)S(1)} %collective-permute-done.3, bf16[2,2048,1024]{2,1,0:T(8,128)(2,1)S(1)} %bitcast.36), kind=kOutput, calls=%fused_computation.31 | convolution fusion | flops 1074266112 | bytes 7340032 | tf_op jit(solution)/shard_map/dot_general | solution.py:33
  194.1 0.0 all-gather.2.cloned.1.call-done
  194.1 0.0 copy-done
  194.2 4.5 %add_convert_fusion = bf16[1024,1024]{1,0:T(8,128)(2,1)} fusion(f32[512,1024]{1,0:T(8,128)} %fusion.33, f32[512,1024]{1,0:T(8,128)S(1)} %fusion.30, bf16[256,1024]{1,0:T(8,128)(2,1)S(1)} %copy-done, f32[1024,256]{1,0:T(8,128)} %all-gather.2.cloned.1.call-done), kind=kOutput, calls=%fused_computation.2 | convolution fusion | flops 544473088 | bytes 7864320 | tf_op jit(solution)/shard_map/dot_general | solution.py:56
  (1 shorter events, 0.0 us)
Async XLA Ops:
  6.5 187.6 %copy-start = (bf16[256,1024]{1,0:T(8,128)(2,1)S(1)}, bf16[256,1024]{1,0:T(8,128)(2,1)}, u32[]{:S(2)}) copy-start(bf16[256,1024]{1,0:T(8,128)(2,1)} %param.7) | copy-start | bytes 1572868
  6.5 5.3 %copy-start.1 = (bf16[1024,1024]{1,0:T(8,128)(2,1)S(1)}, bf16[1024,1024]{1,0:T(8,128)(2,1)}, u32[]{:S(2)}) copy-start(bf16[1024,1024]{1,0:T(8,128)(2,1)} %param.4) | copy-start | bytes 6291460
  6.5 5.3 %copy-start.2 = (bf16[1024,256]{1,0:T(8,128)(2,1)S(1)}, bf16[1024,256]{1,0:T(8,128)(2,1)}, u32[]{:S(2)}) copy-start(bf16[1024,256]{1,0:T(8,128)(2,1)} %param.6) | copy-start | bytes 1572868
  6.5 86.4 %reduce-scatter.2.cloned.1.call-start = ((), (), s32[]{:S(2)}) async-start(), calls=%async_computation.1 | async-start | bytes 1114112 | tf_op jit(solution)/shard_map/reduce_scatter | solution.py:15
  9.7 24.8 %collective-permute-start = (bf16[512,1024]{1,0:T(8,128)(2,1)}, bf16[512,1024]{1,0:T(8,128)(2,1)}, u32[]{:S(2)}, u32[]{:S(2)}) collective-permute-start(bf16[512,1024]{1,0:T(8,128)(2,1)} %get-tuple-element.7), channel_id=1, source_target_pairs={{0,16},{16,0},{32,48},{48,32},{64,80},{80,64},{96,112},{112,96},{1... | collective-permute-start | bytes 3145736 | tf_op jit(solution)/shard_map/ppermute | solution.py:27
  11.8 49.8 %collective-permute-start.1 = (bf16[512,1024]{1,0:T(8,128)(2,1)}, bf16[512,1024]{1,0:T(8,128)(2,1)}, u32[]{:S(2)}, u32[]{:S(2)}) collective-permute-start(bf16[512,1024]{1,0:T(8,128)(2,1)} %get-tuple-element.8), channel_id=1, source_target_pairs={{0,16},{16,0},{32,48},{48,32},{64,80},{80,64},{96,112},{112,96},{1... | collective-permute-start | bytes 3145736 | tf_op jit(solution)/shard_map/ppermute | solution.py:27
  13.6 180.6 %all-gather.2.cloned.1.call-start = ((), (), s32[]{:S(2)}) async-start(), calls=%async_computation.2 | async-start | bytes 1114112 | tf_op jit(solution)/shard_map/all_gather | solution.py:16
  93.2 73.2 %collective-permute-start.2 = (bf16[512,1024]{1,0:T(8,128)(2,1)S(1)}, bf16[512,1024]{1,0:T(8,128)(2,1)S(1)}, u32[]{:S(2)}, u32[]{:S(2)}) collective-permute-start(bf16[512,1024]{1,0:T(8,128)(2,1)S(1)} %get-tuple-element.5), channel_id=1, source_target_pairs={{0,128},{128,0},{16,144},{144,16},{32,160},{160,32},{48,176},{176,... | collective-permute-start | bytes 3145736 | tf_op jit(solution)/shard_map/ppermute | solution.py:27
  93.3 98.3 %collective-permute-start.3 = (bf16[512,1024]{1,0:T(8,128)(2,1)S(1)}, bf16[512,1024]{1,0:T(8,128)(2,1)S(1)}, u32[]{:S(2)}, u32[]{:S(2)}) collective-permute-start(bf16[512,1024]{1,0:T(8,128)(2,1)S(1)} %get-tuple-element.6), channel_id=1, source_target_pairs={{0,128},{128,0},{16,144},{144,16},{32,160},{160,32},{48,176},{176,... | collective-permute-start | bytes 3145736 | tf_op jit(solution)/shard_map/ppermute | solution.py:27
  95.6 70.8 %slice-start = ((s8[8388608]{0:T(1024)(128)(4,1)}), s8[4194304]{0:T(1024)(128)(4,1)S(1)}, s32[]{:S(2)}) async-start(s8[8388608]{0:T(1024)(128)(4,1)} %bitcast.35), calls=%async_computation.3 | async-start | bytes 8388608
  98.6 67.8 %slice-start.1 = ((s8[8388608]{0:T(1024)(128)(4,1)}), s8[4194304]{0:T(1024)(128)(4,1)S(1)}, s32[]{:S(2)}) async-start(s8[8388608]{0:T(1024)(128)(4,1)} %bitcast.35), calls=%async_computation.4 | async-start | bytes 8388608
Sparse Core Ops, SparseCore 0:
  13.7 79.2 reduce-scatter.1
  94.7 82.2 all-gather.1
where the time goes:
time: 206 us; the launch traced here: 205 us
  waiting for transfers between devices  155 us (75%)
  matrix products  28.1 us (14%)
  between operations  13.5 us (7%)
  starting transfers between devices  4.62 us (2%)
  local copies, waits for them, and re-layouts  3.38 us (2%)
    ppermute x4, waiting for transfers between devices, swapped(): return lax.ppermute(block, axis, route)  128 us
    reduce_scatter x1, waiting for transfers between devices, sum_by_parts(): own = lax.psum_scatter(padded, axis, scatter_dimension=0, tiled=True)  27 us
    dot_general x4, matrix products, pair_product(): jnp.dot(own_rows, section_weight[:block_width], preferred_element_type=jn...  11.7 us
    dot_general x4, matrix products, pair_product(): jnp.dot(partner_rows, section_weight[block_width:], preferred_element_typ...  10.3 us
    ppermute x4, starting transfers between devices, swapped(): return lax.ppermute(block, axis, route)  4.58 us
    dot_general x1, matrix products, on_device(): jnp.dot(rank_total.astype(jnp.bfloat16), rank_up, preferred_element_type=...  4.48 us
  transfers between devices with their start and end apart: 6, of which 5 were waited for; matrix products, arithmetic and copies ran while one was open for 12% of the time, Pallas kernels for 0%

commit v1 on v0

v1 whole, which is shorter than its diff:
```python
import jax
import jax.numpy as jnp
from jax import lax
from jax.sharding import PartitionSpec as P

ROWS = (64, 128, 128, 128, 128, 128, 128, 128, 64)
BOUNDS = tuple((sum(ROWS[:i]), sum(ROWS[: i + 1])) for i in range(len(ROWS)))
LAST = len(ROWS) - 1
PIECES = 4


def exchanged(block, stride):
    count = lax.axis_size("feat")
    return lax.ppermute(block, "feat", [(i, i ^ stride) for i in range(count)])


def product(left, right):
    return jnp.dot(left, right, preferred_element_type=jnp.float32)


def halves(block, bit):
    half = block.shape[0] // 2
    kept = lax.dynamic_slice_in_dim(block, bit * half, half, 0)
    sent = lax.dynamic_slice_in_dim(block, (1 - bit) * half, half, 0)
    return kept, sent


def layer(tokens, pair_weights, rank_down, rank_up):
    width = tokens.shape[1]
    far = lax.axis_size("feat") // 2
    me = lax.axis_index("feat")
    b0, b1 = me & 1, (me >> 1) & 1
    mine = b1 * 2 + (b0 ^ b1)
    chunks = range(len(ROWS))

    w_own, w_other = pair_weights[0, :width], pair_weights[0, width:]
    n_own, n_other = pair_weights[1, :width], pair_weights[1, width:]

    def cut(source, k):
        return lax.slice_in_dim(source, *BOUNDS[k], axis=0)

    def after(done, k):
        source, done = lax.optimization_barrier((tokens, done))
        return cut(source, k), done

    rows, partner, own, state, received = [cut(tokens, 0)], [], [], [], []
    for k in chunks:
        if k == 1:
            chunk, own[0] = after(own[0], k)
            rows.append(chunk)
        elif k > 1:
            chunk, partner[k - 2] = after(partner[k - 2], k)
            rows.append(chunk)
        partner.append(exchanged(rows[k], 1))
        own.append(lax.optimization_barrier(product(rows[k], w_own)))
    for k in chunks:
        state.append(jax.nn.silu(own[k] + product(partner[k], w_other)).astype(jnp.bfloat16))
    for k in chunks:
        received.append(exchanged(state[k], far))

    kept, sent = halves(product(tokens, rank_down), b1)
    sent = sent.astype(jnp.bfloat16)
    for stride, bit in ((3, b0 ^ b1), (1, None)):
        got = exchanged(sent, stride)
        partial = kept + got.astype(jnp.float32)
        if bit is not None:
            kept, sent = halves(partial, bit)
    got = exchanged(partial, 4)
    partial = lax.optimization_barrier(partial + got)
    sent = partial.astype(jnp.bfloat16)
    got = exchanged(sent, far)
    low = (partial + got.astype(jnp.float32)).astype(jnp.bfloat16)
    got = exchanged(low, 1)
    low = jnp.concatenate([low, got], 0)
    got = exchanged(low, 3)
    low = jnp.concatenate([low, got], 0)
    piece = tokens.shape[0] // PIECES

    out = jnp.zeros(tokens.shape, jnp.bfloat16)
    for k, (a, b) in enumerate(BOUNDS):
        parts = []
        while a < b:
            block, offset = divmod(a, piece)
            size = min(b, (block + 1) * piece) - a
            parts.append(lax.dynamic_slice_in_dim(low, (block ^ mine) * piece + offset, size, 0))
            a += size
        side = product(jnp.concatenate(parts, 0), rank_up)
        side = lax.optimization_barrier(side)
        pre = lax.optimization_barrier(product(state[k], n_own))
        done = jax.nn.silu(pre + product(received[k], n_other))
        if k < LAST - 1:
            done = lax.optimization_barrier(done)
        out = lax.dynamic_update_slice_in_dim(out, (done + side).astype(jnp.bfloat16), BOUNDS[k][0], 0)
    return out


def solution(mesh):
    return jax.shard_map(
        layer,
        mesh=mesh,
        in_specs=(P("tok", "feat"), P(None, None, "feat"), P("feat", None), P(None, "feat")),
        out_specs=P("tok", "feat"),
        check_vma=False,
    )
```

time: 206 us -> 126 us (0.61)
  waiting for transfers between devices: 155 us -> 52.6 us
  starting transfers between devices: 4.62 us -> 33.9 us
  between operations: 13.5 us -> 0.69 us
  matrix products: 28.1 us -> 33.2 us
    ppermute x4 -> x24, waiting for transfers between devices: 128 us -> 52.6 us  [exchanged(): return lax.ppermute(block, 'feat', [(i, i ^ stride) for i in range(count)])]
    ppermute x4 -> x24, starting transfers between devices: 4.58 us -> 33.9 us  [exchanged(): return lax.ppermute(block, 'feat', [(i, i ^ stride) for i in range(count)])]
    reduce_scatter x1 -> x0, waiting for transfers between devices: 27 us -> none  [sum_by_parts(): own = lax.psum_scatter(padded, axis, scatter_dimension=0, tiled=True)]
    dot_general x10 -> x46, matrix products: 28.1 us -> 33.2 us  [product(): return jnp.dot(left, right, preferred_element_type=jnp.float32)]
    slice x2 -> x9, local copies, waits for them, and re-layouts: 3.35 us -> 0.15 us  [cut(): return lax.slice_in_dim(source, *BOUNDS[k], axis=0)]
    unnamed x10 -> x16, local copies, waits for them, and re-layouts: 0.02 us -> 2.93 us
  transfers between devices with their start and end apart: 6 -> 24, of which waited for: 5 -> 8; matrix products, arithmetic and copies ran while one was open for 12% -> 25% of each run, Pallas kernels for 0% -> 0%
where the time goes in v1:
time: 126 us; the launch traced here: 125 us
  waiting for transfers between devices  52.6 us (42%)
  starting transfers between devices  33.9 us (27%)
  matrix products  33.2 us (26%)
  local copies, waits for them, and re-layouts  3.41 us (3%)
  other arithmetic  1.55 us (1%)
    ppermute x24, waiting for transfers between devices, exchanged(): return lax.ppermute(block, 'feat', [(i, i ^ stride) for i in range(count)])  52.6 us
    ppermute x24, starting transfers between devices, exchanged(): return lax.ppermute(block, 'feat', [(i, i ^ stride) for i in range(count)])  33.9 us
    dot_general x46, matrix products, product(): return jnp.dot(left, right, preferred_element_type=jnp.float32)  33.2 us
    unnamed x16, local copies, waits for them, and re-layouts  2.93 us
  transfers between devices with their start and end apart: 24, of which 8 were waited for; matrix products, arithmetic and copies ran while one was open for 25% of the time, Pallas kernels for 0%

profile of v1, /device:TPU:1, one launch (start us, length us, event | category | flops | bytes accessed | tf_op | source)
XLA Modules:
  0.0 125.3 jit_solution(13312454469905743901)
XLA Ops:
  0.0 2.5 %fusion.244 = f32[1024,256]{1,0:T(8,128)S(1)} fusion(bf16[1024,1024]{1,0:T(8,128)(2,1)} %param.4, bf16[1024,256]{1,0:T(8,128)(2,1)} %param.6), kind=kOutput, calls=%fused_computation.214 | convolution fusion | flops 536870912 | bytes 3670016 | tf_op jit(solution)/shard_map/dot_general | solution.py:18
  2.6 1.0 copy-done.3
  3.5 3.6 %collective-permute-start.2 = (bf16[512,256]{1,0:T(8,128)(2,1)S(1)}, bf16[512,256]{1,0:T(8,128)(2,1)S(1)}, u32[]{:S(2)}, u32[]{:S(2)}) collective-permute-start(bf16[512,256]{1,0:T(8,128)(2,1)S(1)} %dynamic-slice_convert_fusion), channel_id=1, source_target_pairs={{0,48},{16,32},{32,16},{48,0},{64,112},{80,96},{96,80},{112,64},{1... | collective-permute-start | bytes 786440 | tf_op jit(solution)/shard_map/ppermute | solution.py:14
  7.3 2.8 %fusion.70 = f32[64,1024]{1,0:T(8,128)} fusion(bf16[2,2048,1024]{2,1,0:T(8,128)(2,1)} %param.5, bf16[1024,1024]{1,0:T(8,128)(2,1)S(1)} %copy-done.1), kind=kOutput, calls=%fused_computation.70 | convolution fusion | flops 134217728 | bytes 2490368 | tf_op jit(solution)/shard_map/dot_general | solution.py:18
  10.1 1.5 %collective-permute-start.8 = (bf16[128,1024]{1,0:T(8,128)(2,1)S(1)}, bf16[128,1024]{1,0:T(8,128)(2,1)}, u32[]{:S(2)}, u32[]{:S(2)}) collective-permute-start(bf16[128,1024]{1,0:T(8,128)(2,1)S(1)} %slice.44), channel_id=1, source_target_pairs={{0,16},{16,0},{32,48},{48,32},{64,80},{80,64},{96,112},{112,96},{1... | collective-permute-start | bytes 786440 | tf_op jit(solution)/shard_map/ppermute | solution.py:14
  11.6 2.8 %fusion.68 = f32[128,1024]{1,0:T(8,128)} fusion(bf16[2,2048,1024]{2,1,0:T(8,128)(2,1)} %param.5, bf16[1024,1024]{1,0:T(8,128)(2,1)S(1)} %copy-done.1), kind=kOutput, calls=%fused_computation.68 | convolution fusion | flops 268435456 | bytes 2883584 | tf_op jit(solution)/shard_map/dot_general | solution.py:18
  14.5 2.3 %multiply_convert_fusion.8 = bf16[64,1024]{1,0:T(8,128)(2,1)S(1)} fusion(f32[64,1024]{1,0:T(8,128)} %fusion.70, bf16[64,1024]{1,0:T(8,128)(2,1)} %collective-permute-done, bf16[2,2048,1024]{2,1,0:T(8,128)(2,1)} %param.5), kind=kOutput, calls=%fused_computation.127 | convolution fusion | flops 134610944 | bytes 2621440 | tf_op jit(solution)/shard_map/dot_general | solution.py:18
  16.8 2.1 %fusion.34 = f32[64,1024]{1,0:T(8,128)S(1)} fusion(bf16[64,1024]{1,0:T(8,128)(2,1)S(1)} %multiply_convert_fusion.8, bf16[2,2048,1024]{2,1,0:T(8,128)(2,1)} %param.5), kind=kOutput, calls=%fused_computation.34 | convolution fusion | flops 134217728 | bytes 2490368 | tf_op jit(solution)/shard_map/dot_general | solution.py:18
  18.9 3.1 %collective-permute-start.1 = (bf16[64,1024]{1,0:T(8,128)(2,1)S(1)}, bf16[64,1024]{1,0:T(8,128)(2,1)S(1)}, u32[]{:S(2)}, u32[]{:S(2)}) collective-permute-start(bf16[64,1024]{1,0:T(8,128)(2,1)S(1)} %multiply_convert_fusion.8), channel_id=1, source_target_pairs={{0,128},{16,144},{32,160},{48,176},{64,192},{80,208},{96,224},{112... | collective-permute-start | bytes 393224 | tf_op jit(solution)/shard_map/ppermute | solution.py:14
  22.1 2.2 %fusion.66 = f32[128,1024]{1,0:T(8,128)S(1)} fusion(bf16[2,2048,1024]{2,1,0:T(8,128)(2,1)} %param.5, bf16[1024,1024]{1,0:T(8,128)(2,1)S(1)} %copy-done.1), kind=kOutput, calls=%fused_computation.66 | convolution fusion | flops 268435456 | bytes 2883584 | tf_op jit(solution)/shard_map/dot_general | solution.py:18
  24.3 2.2 %multiply_convert_fusion.6 = bf16[128,1024]{1,0:T(8,128)(2,1)S(1)} fusion(f32[128,1024]{1,0:T(8,128)S(1)} %copy-done.5, bf16[128,1024]{1,0:T(8,128)(2,1)} %collective-permute-done.8, bf16[2,2048,1024]{2,1,0:T(8,128)(2,1)} %param.5), kind=kOutput, calls=%fused_computation.110 | convolution fusion | flops 269221888 | bytes 3145728 | tf_op jit(solution)/shard_map/dot_general | solution.py:18
  26.6 0.4 fusion.32
  27.1 0.6 copy-done.4
  27.8 1.4 %collective-permute-start.3 = (f32[256,256]{1,0:T(8,128)S(1)}, f32[256,256]{1,0:T(8,128)S(1)}, u32[]{:S(2)}, u32[]{:S(2)}) collective-permute-start(f32[256,256]{1,0:T(8,128)S(1)} %constant_dynamic-slice_fusion.6), channel_id=1, source_target_pairs={{0,16},{16,0},{32,48},{48,32},{64,80},{80,64},{96,112},{112,96},{1... | collective-permute-start | bytes 786440 | tf_op jit(solution)/shard_map/ppermute | solution.py:14
  29.2 0.5 divide_multiply_fusion.6
  30.0 0.4 fusion.64
  30.5 0.5 multiply_convert_fusion.5
  31.0 0.4 fusion.30
  31.4 1.8 %collective-permute-start.11 = (bf16[128,1024]{1,0:T(8,128)(2,1)S(1)}, bf16[128,1024]{1,0:T(8,128)(2,1)S(1)}, u32[]{:S(2)}, u32[]{:S(2)}) collective-permute-start(bf16[128,1024]{1,0:T(8,128)(2,1)S(1)} %multiply_convert_fusion.5), channel_id=1, source_target_pairs={{0,128},{16,144},{32,160},{48,176},{64,192},{80,208},{96,224},{112... | collective-permute-start | bytes 786440 | tf_op jit(solution)/shard_map/ppermute | solution.py:14
  33.2 0.4 fusion.62
  33.7 1.4 %collective-permute-start.14 = (bf16[128,1024]{1,0:T(8,128)(2,1)S(1)}, bf16[128,1024]{1,0:T(8,128)(2,1)S(1)}, u32[]{:S(2)}, u32[]{:S(2)}) collective-permute-start(bf16[128,1024]{1,0:T(8,128)(2,1)S(1)} %slice.47), channel_id=1, source_target_pairs={{0,16},{16,0},{32,48},{48,32},{64,80},{80,64},{96,112},{112,96},{1... | collective-permute-start | bytes 786440 | tf_op jit(solution)/shard_map/ppermute | solution.py:14
  35.1 6.5 %collective-permute-start.4 = (f32[256,256]{1,0:T(8,128)S(1)}, f32[256,256]{1,0:T(8,128)S(1)}, u32[]{:S(2)}, u32[]{:S(2)}) collective-permute-start(f32[256,256]{1,0:T(8,128)S(1)} %dynamic-slice_add_fusion), channel_id=1, source_target_pairs={{0,64},{16,80},{32,96},{48,112},{64,0},{80,16},{96,32},{112,48},{1... | collective-permute-start | bytes 786440 | tf_op jit(solution)/shard_map/ppermute | solution.py:14
  41.6 0.5 multiply_convert_fusion.4
  42.4 0.4 fusion.28
  42.9 0.5 divide_multiply_fusion.5
  43.4 0.5 collective-permute-start.16
  43.9 0.4 fusion.60
  44.4 0.7 collective-permute-done.14
  45.1 0.5 multiply_convert_fusion.3
  45.6 1.5 %collective-permute-start.15 = (bf16[128,1024]{1,0:T(8,128)(2,1)S(1)}, bf16[128,1024]{1,0:T(8,128)(2,1)S(1)}, u32[]{:S(2)}, u32[]{:S(2)}) collective-permute-start(bf16[128,1024]{1,0:T(8,128)(2,1)S(1)} %multiply_convert_fusion.3), channel_id=1, source_target_pairs={{0,128},{16,144},{32,160},{48,176},{64,192},{80,208},{96,224},{112... | collective-permute-start | bytes 786440 | tf_op jit(solution)/shard_map/ppermute | solution.py:14
  47.1 0.4 fusion.26
  47.6 6.6 %collective-permute-done.11 = bf16[128,1024]{1,0:T(8,128)(2,1)S(1)} collective-permute-done((bf16[128,1024]{1,0:T(8,128)(2,1)S(1)}, bf16[128,1024]{1,0:T(8,128)(2,1)S(1)}, u32[]{:S(2)}, u32[]{:S(2)}) %collective-permute-start.11) | collective-permute-done | bytes 262176 | tf_op jit(solution)/shard_map/ppermute | solution.py:14
  54.1 0.5 divide_multiply_fusion.4
  54.6 1.8 %collective-permute-start.18 = (bf16[128,1024]{1,0:T(8,128)(2,1)S(1)}, bf16[128,1024]{1,0:T(8,128)(2,1)S(1)}, u32[]{:S(2)}, u32[]{:S(2)}) collective-permute-start(bf16[128,1024]{1,0:T(8,128)(2,1)S(1)} %slice.49), channel_id=1, source_target_pairs={{0,16},{16,0},{32,48},{48,32},{64,80},{80,64},{96,112},{112,96},{1... | collective-permute-start | bytes 786440 | tf_op jit(solution)/shard_map/ppermute | solution.py:14
  56.5 0.4 fusion.58
  57.1 0.5 multiply_convert_fusion.2
  57.6 2.4 %collective-permute-start.17 = (bf16[128,1024]{1,0:T(8,128)(2,1)S(1)}, bf16[128,1024]{1,0:T(8,128)(2,1)S(1)}, u32[]{:S(2)}, u32[]{:S(2)}) collective-permute-start(bf16[128,1024]{1,0:T(8,128)(2,1)S(1)} %multiply_convert_fusion.2), channel_id=1, source_target_pairs={{0,128},{16,144},{32,160},{48,176},{64,192},{80,208},{96,224},{112... | collective-permute-start | bytes 786440 | tf_op jit(solution)/shard_map/ppermute | solution.py:14
  60.1 0.4 fusion.24
  60.5 7.6 %collective-permute-done.13 = bf16[128,1024]{1,0:T(8,128)(2,1)S(1)} collective-permute-done((bf16[128,1024]{1,0:T(8,128)(2,1)S(1)}, bf16[128,1024]{1,0:T(8,128)(2,1)S(1)}, u32[]{:S(2)}, u32[]{:S(2)}) %collective-permute-start.13) | collective-permute-done | bytes 262176 | tf_op jit(solution)/shard_map/ppermute | solution.py:14
  68.2 0.5 divide_multiply_fusion.3
  68.7 0.4 fusion.56
  69.2 1.4 %collective-permute-start.20 = (bf16[128,1024]{1,0:T(8,128)(2,1)S(1)}, bf16[128,1024]{1,0:T(8,128)(2,1)S(1)}, u32[]{:S(2)}, u32[]{:S(2)}) collective-permute-start(bf16[128,1024]{1,0:T(8,128)(2,1)S(1)} %slice.50), channel_id=1, source_target_pairs={{0,16},{16,0},{32,48},{48,32},{64,80},{80,64},{96,112},{112,96},{1... | collective-permute-start | bytes 786440 | tf_op jit(solution)/shard_map/ppermute | solution.py:14
  70.5 14.5 %collective-permute-done.5 = bf16[256,256]{1,0:T(8,128)(2,1)S(1)} collective-permute-done((bf16[256,256]{1,0:T(8,128)(2,1)S(1)}, bf16[256,256]{1,0:T(8,128)(2,1)S(1)}, u32[]{:S(2)}, u32[]{:S(2)}) %collective-permute-start.5) | collective-permute-done | bytes 131104 | tf_op jit(solution)/shard_map/ppermute | solution.py:14
  85.0 1.4 %collective-permute-start.6 = (bf16[256,256]{1,0:T(8,128)(2,1)S(1)}, bf16[256,256]{1,0:T(8,128)(2,1)S(1)}, u32[]{:S(2)}, u32[]{:S(2)}) collective-permute-start(bf16[256,256]{1,0:T(8,128)(2,1)S(1)} %add_convert_fusion.9), channel_id=1, source_target_pairs={{0,16},{16,0},{32,48},{48,32},{64,80},{80,64},{96,112},{112,96},{1... | collective-permute-start | bytes 393224 | tf_op jit(solution)/shard_map/ppermute | solution.py:14
  86.4 0.5 multiply_convert_fusion.1
  87.0 0.4 fusion.22
  87.5 0.5 divide_multiply_fusion.2
  88.0 0.5 fusion.54
  88.8 0.5 collective-permute-done.6
  89.3 0.8 collective-permute-start.7
  90.1 0.5 multiply_convert_fusion
  90.6 2.2 %collective-permute-start.21 = (bf16[128,1024]{1,0:T(8,128)(2,1)S(1)}, bf16[128,1024]{1,0:T(8,128)(2,1)S(1)}, u32[]{:S(2)}, u32[]{:S(2)}) collective-permute-start(bf16[128,1024]{1,0:T(8,128)(2,1)S(1)} %multiply_convert_fusion), channel_id=1, source_target_pairs={{0,128},{16,144},{32,160},{48,176},{64,192},{80,208},{96,224},{112... | collective-permute-start | bytes 786440 | tf_op jit(solution)/shard_map/ppermute | solution.py:14
  92.8 1.1 collective-permute-done.22
  93.8 0.5 multiply_convert_fusion.7
  94.4 1.3 %collective-permute-start.23 = (bf16[64,1024]{1,0:T(8,128)(2,1)S(1)}, bf16[64,1024]{1,0:T(8,128)(2,1)S(1)}, u32[]{:S(2)}, u32[]{:S(2)}) collective-permute-start(bf16[64,1024]{1,0:T(8,128)(2,1)S(1)} %multiply_convert_fusion.7), channel_id=1, source_target_pairs={{0,128},{16,144},{32,160},{48,176},{64,192},{80,208},{96,224},{112... | collective-permute-start | bytes 393224 | tf_op jit(solution)/shard_map/ppermute | solution.py:14
  96.1 8.5 %collective-permute-done.17 = bf16[128,1024]{1,0:T(8,128)(2,1)S(1)} collective-permute-done((bf16[128,1024]{1,0:T(8,128)(2,1)S(1)}, bf16[128,1024]{1,0:T(8,128)(2,1)S(1)}, u32[]{:S(2)}, u32[]{:S(2)}) %collective-permute-start.17) | collective-permute-done | bytes 262176 | tf_op jit(solution)/shard_map/ppermute | solution.py:14
  104.7 0.5 divide_multiply_fusion.1
  105.2 0.5 fusion.18
  105.7 13.0 %collective-permute-done.23 = bf16[64,1024]{1,0:T(8,128)(2,1)S(1)} collective-permute-done((bf16[64,1024]{1,0:T(8,128)(2,1)S(1)}, bf16[64,1024]{1,0:T(8,128)(2,1)S(1)}, u32[]{:S(2)}, u32[]{:S(2)}) %collective-permute-start.23) | collective-permute-done | bytes 131104 | tf_op jit(solution)/shard_map/ppermute | solution.py:14
  118.7 0.5 fusion.123
  119.2 0.5 divide_multiply_fusion
  122.7 0.5 fusion.111
  123.3 1.3 %copy-done.2 = bf16[1024,1024]{1,0:T(8,128)(2,1)} copy-done((bf16[1024,1024]{1,0:T(8,128)(2,1)}, bf16[1024,1024]{1,0:T(8,128)(2,1)S(1)}, u32[]{:S(2)}) %copy-start.2) | copy-done | bytes 2097176
  124.6 0.7 fusion.165
  (76 shorter events, 5.2 us)
Async XLA Ops:
  0.0 119.8 %copy-start = (bf16[256,1024]{1,0:T(8,128)(2,1)S(1)}, bf16[256,1024]{1,0:T(8,128)(2,1)}, u32[]{:S(2)}) copy-start(bf16[256,1024]{1,0:T(8,128)(2,1)} %param.7) | copy-start | bytes 1572868
  0.0 7.2 %copy-start.1 = (bf16[1024,1024]{1,0:T(8,128)(2,1)S(1)}, bf16[1024,1024]{1,0:T(8,128)(2,1)}, u32[]{:S(2)}) copy-start(bf16[1024,1024]{1,0:T(8,128)(2,1)} %param.4) | copy-start | bytes 6291460
  2.5 1.0 copy-start.3
  3.5 23.5 %collective-permute-start.2 = (bf16[512,256]{1,0:T(8,128)(2,1)S(1)}, bf16[512,256]{1,0:T(8,128)(2,1)S(1)}, u32[]{:S(2)}, u32[]{:S(2)}) collective-permute-start(bf16[512,256]{1,0:T(8,128)(2,1)S(1)} %dynamic-slice_convert_fusion), channel_id=1, source_target_pairs={{0,48},{16,32},{32,16},{48,0},{64,112},{80,96},{96,80},{112,64},{1... | collective-permute-start | bytes 786440 | tf_op jit(solution)/shard_map/ppermute | solution.py:14
  7.2 7.3 %collective-permute-start = (bf16[64,1024]{1,0:T(8,128)(2,1)S(1)}, bf16[64,1024]{1,0:T(8,128)(2,1)}, u32[]{:S(2)}, u32[]{:S(2)}) collective-permute-start(bf16[64,1024]{1,0:T(8,128)(2,1)S(1)} %slice.39), channel_id=1, source_target_pairs={{0,16},{16,0},{32,48},{48,32},{64,80},{80,64},{96,112},{112,96},{1... | collective-permute-start | bytes 393224 | tf_op jit(solution)/shard_map/ppermute | solution.py:14
  10.1 14.2 %collective-permute-start.8 = (bf16[128,1024]{1,0:T(8,128)(2,1)S(1)}, bf16[128,1024]{1,0:T(8,128)(2,1)}, u32[]{:S(2)}, u32[]{:S(2)}) collective-permute-start(bf16[128,1024]{1,0:T(8,128)(2,1)S(1)} %slice.44), channel_id=1, source_target_pairs={{0,16},{16,0},{32,48},{48,32},{64,80},{80,64},{96,112},{112,96},{1... | collective-permute-start | bytes 786440 | tf_op jit(solution)/shard_map/ppermute | solution.py:14
  14.5 12.1 %slice-start = ((s8[8388608]{0:T(1024)(128)(4,1)}), s8[4194304]{0:T(1024)(128)(4,1)S(1)}, s32[]{:S(2)}) async-start(s8[8388608]{0:T(1024)(128)(4,1)} %bitcast.182), calls=%async_computation | async-start | bytes 8388608
  18.9 5.4 %copy-start.5 = (f32[128,1024]{1,0:T(8,128)S(1)}, f32[128,1024]{1,0:T(8,128)}, u32[]{:S(2)}) copy-start(f32[128,1024]{1,0:T(8,128)} %fusion.68) | copy-start | bytes 1572868
  18.9 10.3 %collective-permute-start.1 = (bf16[64,1024]{1,0:T(8,128)(2,1)S(1)}, bf16[64,1024]{1,0:T(8,128)(2,1)S(1)}, u32[]{:S(2)}, u32[]{:S(2)}) collective-permute-start(bf16[64,1024]{1,0:T(8,128)(2,1)S(1)} %multiply_convert_fusion.8), channel_id=1, source_target_pairs={{0,128},{16,144},{32,160},{48,176},{64,192},{80,208},{96,224},{112... | collective-permute-start | bytes 393224 | tf_op jit(solution)/shard_map/ppermute | solution.py:14
  22.0 4.6 %slice-start.1 = ((s8[8388608]{0:T(1024)(128)(4,1)}), s8[4194304]{0:T(1024)(128)(4,1)S(1)}, s32[]{:S(2)}) async-start(s8[8388608]{0:T(1024)(128)(4,1)} %bitcast.182), calls=%async_computation.1 | async-start | bytes 8388608
  22.0 8.5 %collective-permute-start.10 = (bf16[128,1024]{1,0:T(8,128)(2,1)S(1)}, bf16[128,1024]{1,0:T(8,128)(2,1)S(1)}, u32[]{:S(2)}, u32[]{:S(2)}) collective-permute-start(bf16[128,1024]{1,0:T(8,128)(2,1)S(1)} %slice.45), channel_id=1, source_target_pairs={{0,16},{16,0},{32,48},{48,32},{64,80},{80,64},{96,112},{112,96},{1... | collective-permute-start | bytes 786440 | tf_op jit(solution)/shard_map/ppermute | solution.py:14
  26.5 1.2 copy-start.4
  26.5 16.4 %collective-permute-start.9 = (bf16[128,1024]{1,0:T(8,128)(2,1)S(1)}, bf16[128,1024]{1,0:T(8,128)(2,1)S(1)}, u32[]{:S(2)}, u32[]{:S(2)}) collective-permute-start(bf16[128,1024]{1,0:T(8,128)(2,1)S(1)} %multiply_convert_fusion.6), channel_id=1, source_target_pairs={{0,128},{16,144},{32,160},{48,176},{64,192},{80,208},{96,224},{112... | collective-permute-start | bytes 786440 | tf_op jit(solution)/shard_map/ppermute | solution.py:14
  27.8 7.3 %collective-permute-start.3 = (f32[256,256]{1,0:T(8,128)S(1)}, f32[256,256]{1,0:T(8,128)S(1)}, u32[]{:S(2)}, u32[]{:S(2)}) collective-permute-start(f32[256,256]{1,0:T(8,128)S(1)} %constant_dynamic-slice_fusion.6), channel_id=1, source_target_pairs={{0,16},{16,0},{32,48},{48,32},{64,80},{80,64},{96,112},{112,96},{1... | collective-permute-start | bytes 786440 | tf_op jit(solution)/shard_map/ppermute | solution.py:14
  29.7 11.9 %collective-permute-start.12 = (bf16[128,1024]{1,0:T(8,128)(2,1)S(1)}, bf16[128,1024]{1,0:T(8,128)(2,1)S(1)}, u32[]{:S(2)}, u32[]{:S(2)}) collective-permute-start(bf16[128,1024]{1,0:T(8,128)(2,1)S(1)} %slice.46), channel_id=1, source_target_pairs={{0,16},{16,0},{32,48},{48,32},{64,80},{80,64},{96,112},{112,96},{1... | collective-permute-start | bytes 786440 | tf_op jit(solution)/shard_map/ppermute | solution.py:14
  31.4 22.7 %collective-permute-start.11 = (bf16[128,1024]{1,0:T(8,128)(2,1)S(1)}, bf16[128,1024]{1,0:T(8,128)(2,1)S(1)}, u32[]{:S(2)}, u32[]{:S(2)}) collective-permute-start(bf16[128,1024]{1,0:T(8,128)(2,1)S(1)} %multiply_convert_fusion.5), channel_id=1, source_target_pairs={{0,128},{16,144},{32,160},{48,176},{64,192},{80,208},{96,224},{112... | collective-permute-start | bytes 786440 | tf_op jit(solution)/shard_map/ppermute | solution.py:14
  33.7 11.3 %collective-permute-start.14 = (bf16[128,1024]{1,0:T(8,128)(2,1)S(1)}, bf16[128,1024]{1,0:T(8,128)(2,1)S(1)}, u32[]{:S(2)}, u32[]{:S(2)}) collective-permute-start(bf16[128,1024]{1,0:T(8,128)(2,1)S(1)} %slice.47), channel_id=1, source_target_pairs={{0,16},{16,0},{32,48},{48,32},{64,80},{80,64},{96,112},{112,96},{1... | collective-permute-start | bytes 786440 | tf_op jit(solution)/shard_map/ppermute | solution.py:14
  35.1 21.8 %collective-permute-start.4 = (f32[256,256]{1,0:T(8,128)S(1)}, f32[256,256]{1,0:T(8,128)S(1)}, u32[]{:S(2)}, u32[]{:S(2)}) collective-permute-start(f32[256,256]{1,0:T(8,128)S(1)} %dynamic-slice_add_fusion), channel_id=1, source_target_pairs={{0,64},{16,80},{32,96},{48,112},{64,0},{80,16},{96,32},{112,48},{1... | collective-permute-start | bytes 786440 | tf_op jit(solution)/shard_map/ppermute | solution.py:14
  42.1 26.0 %collective-permute-start.13 = (bf16[128,1024]{1,0:T(8,128)(2,1)S(1)}, bf16[128,1024]{1,0:T(8,128)(2,1)S(1)}, u32[]{:S(2)}, u32[]{:S(2)}) collective-permute-start(bf16[128,1024]{1,0:T(8,128)(2,1)S(1)} %multiply_convert_fusion.4), channel_id=1, source_target_pairs={{0,128},{16,144},{32,160},{48,176},{64,192},{80,208},{96,224},{112... | collective-permute-start | bytes 786440 | tf_op jit(solution)/shard_map/ppermute | solution.py:14
  43.4 13.7 %collective-permute-start.16 = (bf16[128,1024]{1,0:T(8,128)(2,1)S(1)}, bf16[128,1024]{1,0:T(8,128)(2,1)S(1)}, u32[]{:S(2)}, u32[]{:S(2)}) collective-permute-start(bf16[128,1024]{1,0:T(8,128)(2,1)S(1)} %slice.48), channel_id=1, source_target_pairs={{0,16},{16,0},{32,48},{48,32},{64,80},{80,64},{96,112},{112,96},{1... | collective-permute-start | bytes 786440 | tf_op jit(solution)/shard_map/ppermute | solution.py:14
  45.6 41.9 %collective-permute-start.15 = (bf16[128,1024]{1,0:T(8,128)(2,1)S(1)}, bf16[128,1024]{1,0:T(8,128)(2,1)S(1)}, u32[]{:S(2)}, u32[]{:S(2)}) collective-permute-start(bf16[128,1024]{1,0:T(8,128)(2,1)S(1)} %multiply_convert_fusion.3), channel_id=1, source_target_pairs={{0,128},{16,144},{32,160},{48,176},{64,192},{80,208},{96,224},{112... | collective-permute-start | bytes 786440 | tf_op jit(solution)/shard_map/ppermute | solution.py:14
  54.6 31.8 %collective-permute-start.18 = (bf16[128,1024]{1,0:T(8,128)(2,1)S(1)}, bf16[128,1024]{1,0:T(8,128)(2,1)S(1)}, u32[]{:S(2)}, u32[]{:S(2)}) collective-permute-start(bf16[128,1024]{1,0:T(8,128)(2,1)S(1)} %slice.49), channel_id=1, source_target_pairs={{0,16},{16,0},{32,48},{48,32},{64,80},{80,64},{96,112},{112,96},{1... | collective-permute-start | bytes 786440 | tf_op jit(solution)/shard_map/ppermute | solution.py:14
  57.0 28.0 %collective-permute-start.5 = (bf16[256,256]{1,0:T(8,128)(2,1)S(1)}, bf16[256,256]{1,0:T(8,128)(2,1)S(1)}, u32[]{:S(2)}, u32[]{:S(2)}) collective-permute-start(bf16[256,256]{1,0:T(8,128)(2,1)S(1)} %convert_element_type.72), channel_id=1, source_target_pairs={{0,128},{16,144},{32,160},{48,176},{64,192},{80,208},{96,224},{112... | collective-permute-start | bytes 393224 | tf_op jit(solution)/shard_map/ppermute | solution.py:14
  57.6 47.0 %collective-permute-start.17 = (bf16[128,1024]{1,0:T(8,128)(2,1)S(1)}, bf16[128,1024]{1,0:T(8,128)(2,1)S(1)}, u32[]{:S(2)}, u32[]{:S(2)}) collective-permute-start(bf16[128,1024]{1,0:T(8,128)(2,1)S(1)} %multiply_convert_fusion.2), channel_id=1, source_target_pairs={{0,128},{16,144},{32,160},{48,176},{64,192},{80,208},{96,224},{112... | collective-permute-start | bytes 786440 | tf_op jit(solution)/shard_map/ppermute | solution.py:14
  69.2 20.9 %collective-permute-start.20 = (bf16[128,1024]{1,0:T(8,128)(2,1)S(1)}, bf16[128,1024]{1,0:T(8,128)(2,1)S(1)}, u32[]{:S(2)}, u32[]{:S(2)}) collective-permute-start(bf16[128,1024]{1,0:T(8,128)(2,1)S(1)} %slice.50), channel_id=1, source_target_pairs={{0,16},{16,0},{32,48},{48,32},{64,80},{80,64},{96,112},{112,96},{1... | collective-permute-start | bytes 786440 | tf_op jit(solution)/shard_map/ppermute | solution.py:14
  85.0 4.2 %collective-permute-start.6 = (bf16[256,256]{1,0:T(8,128)(2,1)S(1)}, bf16[256,256]{1,0:T(8,128)(2,1)S(1)}, u32[]{:S(2)}, u32[]{:S(2)}) collective-permute-start(bf16[256,256]{1,0:T(8,128)(2,1)S(1)} %add_convert_fusion.9), channel_id=1, source_target_pairs={{0,16},{16,0},{32,48},{48,32},{64,80},{80,64},{96,112},{112,96},{1... | collective-permute-start | bytes 393224 | tf_op jit(solution)/shard_map/ppermute | solution.py:14
  86.9 32.3 %collective-permute-start.19 = (bf16[128,1024]{1,0:T(8,128)(2,1)S(1)}, bf16[128,1024]{1,0:T(8,128)(2,1)S(1)}, u32[]{:S(2)}, u32[]{:S(2)}) collective-permute-start(bf16[128,1024]{1,0:T(8,128)(2,1)S(1)} %multiply_convert_fusion.1), channel_id=1, source_target_pairs={{0,128},{16,144},{32,160},{48,176},{64,192},{80,208},{96,224},{112... | collective-permute-start | bytes 786440 | tf_op jit(solution)/shard_map/ppermute | solution.py:14
  88.5 5.3 %collective-permute-start.22 = (bf16[64,1024]{1,0:T(8,128)(2,1)S(1)}, bf16[64,1024]{1,0:T(8,128)(2,1)S(1)}, u32[]{:S(2)}, u32[]{:S(2)}) collective-permute-start(bf16[64,1024]{1,0:T(8,128)(2,1)S(1)} %slice.51), channel_id=1, source_target_pairs={{0,16},{16,0},{32,48},{48,32},{64,80},{80,64},{96,112},{112,96},{1... | collective-permute-start | bytes 393224 | tf_op jit(solution)/shard_map/ppermute | solution.py:14
  89.3 30.5 %collective-permute-start.7 = (bf16[512,256]{1,0:T(8,128)(2,1)S(1)}, bf16[512,256]{1,0:T(8,128)(2,1)S(1)}, u32[]{:S(2)}, u32[]{:S(2)}) collective-permute-start(bf16[512,256]{1,0:T(8,128)(2,1)S(1)} %pad_maximum_fusion.1), channel_id=1, source_target_pairs={{0,48},{16,32},{32,16},{48,0},{64,112},{80,96},{96,80},{112,64},{1... | collective-permute-start | bytes 786440 | tf_op jit(solution)/shard_map/ppermute | solution.py:14
  90.6 32.1 %collective-permute-start.21 = (bf16[128,1024]{1,0:T(8,128)(2,1)S(1)}, bf16[128,1024]{1,0:T(8,128)(2,1)S(1)}, u32[]{:S(2)}, u32[]{:S(2)}) collective-permute-start(bf16[128,1024]{1,0:T(8,128)(2,1)S(1)} %multiply_convert_fusion), channel_id=1, source_target_pairs={{0,128},{16,144},{32,160},{48,176},{64,192},{80,208},{96,224},{112... | collective-permute-start | bytes 786440 | tf_op jit(solution)/shard_map/ppermute | solution.py:14
  94.4 24.3 %collective-permute-start.23 = (bf16[64,1024]{1,0:T(8,128)(2,1)S(1)}, bf16[64,1024]{1,0:T(8,128)(2,1)S(1)}, u32[]{:S(2)}, u32[]{:S(2)}) collective-permute-start(bf16[64,1024]{1,0:T(8,128)(2,1)S(1)} %multiply_convert_fusion.7), channel_id=1, source_target_pairs={{0,128},{16,144},{32,160},{48,176},{64,192},{80,208},{96,224},{112... | collective-permute-start | bytes 393224 | tf_op jit(solution)/shard_map/ppermute | solution.py:14
  123.3 1.3 %copy-start.2 = (bf16[1024,1024]{1,0:T(8,128)(2,1)}, bf16[1024,1024]{1,0:T(8,128)(2,1)S(1)}, u32[]{:S(2)}) copy-start(bf16[1024,1024]{1,0:T(8,128)(2,1)S(1)} %fusion.158) | copy-start | bytes 6291460

commit v2 on v1

--- a/solution.py
+++ b/solution.py
@@ -1,12 +1,16 @@
 import jax
 import jax.numpy as jnp
 from jax import lax
+from jax.experimental import pallas as pl
+from jax.experimental.pallas import tpu as pltpu
 from jax.sharding import PartitionSpec as P
 
 ROWS = (64, 128, 128, 128, 128, 128, 128, 128, 64)
 BOUNDS = tuple((sum(ROWS[:i]), sum(ROWS[: i + 1])) for i in range(len(ROWS)))
 LAST = len(ROWS) - 1
-PIECES = 4
+PIECES = 8
+OPENING = 2
+FAST = 2
 
 
 def exchanged(block, stride):
@@ -16,6 +20,45 @@
 
 def product(left, right):
     return jnp.dot(left, right, preferred_element_type=jnp.float32)
+
+
+def opening(tokens, weights, sizes):
+    width = tokens.shape[1]
+    rows = sum(sizes)
+
+    def body(t_ref, w_ref, *refs):
+        *own_refs, other_ref, rows_ref, own_w_ref, sems = refs
+        copies = [
+            pltpu.make_async_copy(t_ref.at[pl.ds(0, rows)], rows_ref, sems.at[0]),
+            pltpu.make_async_copy(w_ref.at[0, pl.ds(0, width)], own_w_ref, sems.at[1]),
+            pltpu.make_async_copy(w_ref.at[0, pl.ds(width, width)], other_ref, sems.at[2]),
+        ]
+        for copy in copies:
+            copy.start()
+        copies[0].wait()
+        copies[1].wait()
+        start = 0
+        for own_ref, size in zip(own_refs, sizes):
+            own_ref[...] = product(rows_ref[pl.ds(start, size)], own_w_ref[...])
+            start += size
+        copies[2].wait()
+
+    return pl.pallas_call(
+        body,
+        out_shape=(
+            *(pltpu.VMEM((size, width), jnp.float32) for size in sizes),
+            pltpu.VMEM((width, width), weights.dtype),
+        ),
+        in_specs=[pl.BlockSpec(memory_space=pl.ANY), pl.BlockSpec(memory_space=pl.ANY)],
+        out_specs=tuple(pl.BlockSpec(memory_space=pltpu.VMEM) for _ in range(len(sizes) + 1)),
+        scratch_shapes=[
+            pltpu.VMEM((rows, width), tokens.dtype),
+            pltpu.VMEM((width, width), weights.dtype),
+            pltpu.SemaphoreType.DMA((3,)),
+        ],
+        compiler_params=pltpu.CompilerParams(vmem_limit_bytes=56 << 20),
+        name="opening",
+    )(tokens, weights)
 
 
 def halves(block, bit):
@@ -29,8 +72,8 @@
     width = tokens.shape[1]
     far = lax.axis_size("feat") // 2
     me = lax.axis_index("feat")
-    b0, b1 = me & 1, (me >> 1) & 1
-    mine = b1 * 2 + (b0 ^ b1)
+    b0, b1, b2 = me & 1, (me >> 1) & 1, (me >> 2) & 1
+    mine = (b1 * 2 + (b0 ^ b1)) * 2 + b2
     chunks = range(len(ROWS))
 
     w_own, w_other = pair_weights[0, :width], pair_weights[0, width:]
@@ -46,30 +89,35 @@
     rows, partner, own, state, received = [cut(tokens, 0)], [], [], [], []
     for k in chunks:
         if k == 1:
-            chunk, own[0] = after(own[0], k)
+            chunk, rank_up = after(rank_up, k)
             rows.append(chunk)
         elif k > 1:
             chunk, partner[k - 2] = after(partner[k - 2], k)
             rows.append(chunk)
         partner.append(exchanged(rows[k], 1))
-        own.append(lax.optimization_barrier(product(rows[k], w_own)))
+        if k == 0:
+            *own, fast_other = opening(tokens, pair_weights, ROWS[:OPENING])
+        elif k >= OPENING:
+            own.append(lax.optimization_barrier(product(rows[k], w_own)))
     for k in chunks:
-        state.append(jax.nn.silu(own[k] + product(partner[k], w_other)).astype(jnp.bfloat16))
+        left = fast_other if k < FAST else w_other
+        state.append(jax.nn.silu(own[k] + product(partner[k], left)).astype(jnp.bfloat16))
     for k in chunks:
         received.append(exchanged(state[k], far))
 
     kept, sent = halves(product(tokens, rank_down), b1)
     sent = sent.astype(jnp.bfloat16)
-    for stride, bit in ((3, b0 ^ b1), (1, None)):
+    for stride, bit in ((3, b0 ^ b1), (1, b2)):
         got = exchanged(sent, stride)
         partial = kept + got.astype(jnp.float32)
-        if bit is not None:
-            kept, sent = halves(partial, bit)
-    got = exchanged(partial, 4)
-    partial = lax.optimization_barrier(partial + got)
+        kept, sent = halves(partial, bit)
+    got = exchanged(sent, 4)
+    partial = lax.optimization_barrier(kept + got)
     sent = partial.astype(jnp.bfloat16)
     got = exchanged(sent, far)
     low = (partial + got.astype(jnp.float32)).astype(jnp.bfloat16)
+    got = exchanged(low, 4)
+    low = jnp.concatenate([low, got], 0)
     got = exchanged(low, 1)
     low = jnp.concatenate([low, got], 0)
     got = exchanged(low, 3)

time: 126 us -> 127 us (level)
  waiting for transfers between devices: 52.6 us -> 60.8 us
  starting transfers between devices: 33.9 us -> 26.7 us
  matrix products: 33.2 us -> 27.5 us
  Pallas kernels: 0 us -> 2.57 us
  local copies, waits for them, and re-layouts: 3.41 us -> 5.69 us
    ppermute x24 -> x25, waiting for transfers between devices: 52.6 us -> 60.8 us  [exchanged(): return lax.ppermute(block, 'feat', [(i, i ^ stride) for i in range(count)])]
    ppermute x24 -> x25, starting transfers between devices: 33.9 us -> 26.7 us  [exchanged(): return lax.ppermute(block, 'feat', [(i, i ^ stride) for i in range(count)])]
    dot_general x46 -> x44, matrix products: 33.2 us -> 27.5 us  [product(): return jnp.dot(left, right, preferred_element_type=jnp.float32)]
    slice x9, local copies, waits for them, and re-layouts: 0.15 us -> 2.76 us  [cut(): return lax.slice_in_dim(source, *BOUNDS[k], axis=0)]
    pallas_call x0 -> x1, Pallas kernels: none -> 2.57 us  [opening(): pl.pallas_call(body, out_shape=(*(pltpu.VMEM((size, width), jnp.float32)...]
    unnamed x16 -> x14, local copies, waits for them, and re-layouts: 2.93 us -> 1.76 us
  transfers between devices with their start and end apart: 24 -> 25, of which waited for: 8 -> 10; matrix products, arithmetic and copies ran while one was open for 25% -> 25% of each run, Pallas kernels for 0% -> 2%
where the time goes in v2:
time: 127 us; the launch traced here: 126 us
  waiting for transfers between devices  60.8 us (48%)
  matrix products  27.5 us (22%)
  starting transfers between devices  26.7 us (21%)
  local copies, waits for them, and re-layouts  5.69 us (4%)
  Pallas kernels  2.57 us (2%)
  other arithmetic  2.32 us (2%)
    ppermute x25, waiting for transfers between devices, exchanged(): return lax.ppermute(block, 'feat', [(i, i ^ stride) for i in range(count)])  60.8 us
    dot_general x44, matrix products, product(): return jnp.dot(left, right, preferred_element_type=jnp.float32)  27.5 us
    ppermute x25, starting transfers between devices, exchanged(): return lax.ppermute(block, 'feat', [(i, i ^ stride) for i in range(count)])  26.7 us
    slice x9, local copies, waits for them, and re-layouts, cut(): return lax.slice_in_dim(source, *BOUNDS[k], axis=0)  2.76 us
    pallas_call x1, Pallas kernels, opening(): pl.pallas_call(body, out_shape=(*(pltpu.VMEM((size, width), jnp.float32)...  2.57 us
  transfers between devices with their start and end apart: 25, of which 10 were waited for; matrix products, arithmetic and copies ran while one was open for 25% of the time, Pallas kernels for 2%

profile of v2, /device:TPU:1, one launch (start us, length us, event | category | flops | bytes accessed | tf_op | source)
XLA Modules:
  0.0 126.4 jit_solution(7974381948404793188)
XLA Ops:
  0.0 1.0 slice.39
  1.0 2.2 %collective-permute-start = (bf16[64,1024]{1,0:T(8,128)(2,1)S(1)}, bf16[64,1024]{1,0:T(8,128)(2,1)}, u32[]{:S(2)}, u32[]{:S(2)}) collective-permute-start(bf16[64,1024]{1,0:T(8,128)(2,1)S(1)} %slice.39), channel_id=1, source_target_pairs={{0,16},{16,0},{32,48},{48,32},{64,80},{80,64},{96,112},{112,96},{1... | collective-permute-start | bytes 393224 | tf_op jit(solution)/shard_map/ppermute | solution.py:18
  3.2 2.4 %fusion.232 = f32[1024,256]{1,0:T(8,128)S(1)} fusion(bf16[1024,1024]{1,0:T(8,128)(2,1)} %t_ref.1, bf16[1024,256]{1,0:T(8,128)(2,1)} %param.6), kind=kOutput, calls=%fused_computation.219 | convolution fusion | flops 536870912 | bytes 3670016 | tf_op jit(solution)/shard_map/dot_general | solution.py:22
  5.6 0.8 dynamic-slice_convert_fusion
  6.4 1.9 %collective-permute-start.2 = (bf16[512,256]{1,0:T(8,128)(2,1)}, bf16[512,256]{1,0:T(8,128)(2,1)}, u32[]{:S(2)}, u32[]{:S(2)}) collective-permute-start(bf16[512,256]{1,0:T(8,128)(2,1)} %dynamic-slice_convert_fusion), channel_id=1, source_target_pairs={{0,48},{16,32},{32,16},{48,0},{64,112},{80,96},{96,80},{112,64},{1... | collective-permute-start | bytes 786440 | tf_op jit(solution)/shard_map/ppermute | solution.py:18
  8.3 1.7 %slice.42 = bf16[128,1024]{1,0:T(8,128)(2,1)} slice(bf16[1024,1024]{1,0:T(8,128)(2,1)} %t_ref.1), slice={[64:192], [0:1024]} | slice | bytes 524288 | tf_op jit(solution)/shard_map/slice | solution.py:83
  10.4 2.6 %opening.1 = (f32[64,1024]{1,0:T(8,128)S(1)}, f32[128,1024]{1,0:T(8,128)S(1)}, bf16[1024,1024]{1,0:T(8,128)(2,1)S(1)}) custom-call(bf16[1024,1024]{1,0:T(8,128)(2,1)} %t_ref.1, bf16[2,2048,1024]{2,1,0:T(8,128)(2,1)} %w_ref.1), custom_call_target="tpu_custom_call" | custom-call | tf_op jit(solution)/shard_map/opening/pallas_call | solution.py:46
  13.1 1.6 %multiply_convert_fusion.8 = bf16[64,1024]{1,0:T(8,128)(2,1)S(1)} fusion(f32[64,1024]{1,0:T(8,128)S(1)} %get-tuple-element.24, bf16[64,1024]{1,0:T(8,128)(2,1)} %collective-permute-done, bf16[1024,1024]{1,0:T(8,128)(2,1)S(1)} %get-tuple-element.26), kind=kOutput, calls=%fused_computation.132 | convolution fusion | flops 134610944 | bytes 2621440 | tf_op jit(solution)/shard_map/dot_general | solution.py:22
  14.7 3.1 %collective-permute-start.1 = (bf16[64,1024]{1,0:T(8,128)(2,1)S(1)}, bf16[64,1024]{1,0:T(8,128)(2,1)S(1)}, u32[]{:S(2)}, u32[]{:S(2)}) collective-permute-start(bf16[64,1024]{1,0:T(8,128)(2,1)S(1)} %multiply_convert_fusion.8), channel_id=1, source_target_pairs={{0,128},{16,144},{32,160},{48,176},{64,192},{80,208},{96,224},{112... | collective-permute-start | bytes 393224 | tf_op jit(solution)/shard_map/ppermute | solution.py:18
  17.8 2.0 %fusion.26 = f32[128,1024]{1,0:T(8,128)S(1)} fusion(bf16[2,2048,1024]{2,1,0:T(8,128)(2,1)} %w_ref.1, bf16[1024,1024]{1,0:T(8,128)(2,1)S(1)} %copy-done.1), kind=kOutput, calls=%fused_computation.26 | convolution fusion | flops 268435456 | bytes 2883584 | tf_op jit(solution)/shard_map/dot_general | solution.py:22
  19.8 2.1 %fusion.62 = f32[64,1024]{1,0:T(8,128)S(1)} fusion(bf16[64,1024]{1,0:T(8,128)(2,1)S(1)} %multiply_convert_fusion.8, bf16[2,2048,1024]{2,1,0:T(8,128)(2,1)} %w_ref.1), kind=kOutput, calls=%fused_computation.62 | convolution fusion | flops 134217728 | bytes 2490368 | tf_op jit(solution)/shard_map/dot_general | solution.py:22
  21.9 1.2 collective-permute-start.11
  23.1 2.2 %divide_multiply_fusion.6 = f32[64,1024]{1,0:T(8,128)S(1)} fusion(f32[64,1024]{1,0:T(8,128)S(1)} %fusion.62, bf16[64,1024]{1,0:T(8,128)(2,1)S(1)} %collective-permute-done.1, bf16[2,2048,1024]{2,1,0:T(8,128)(2,1)} %w_ref.1), kind=kOutput, calls=%fused_computation.131 | convolution fusion | flops 134545408 | bytes 2752512 | tf_op jit(solution)/shard_map/dot_general | solution.py:22
  25.3 1.4 %multiply_convert_fusion.6 = bf16[128,1024]{1,0:T(8,128)(2,1)S(1)} fusion(f32[128,1024]{1,0:T(8,128)S(1)} %get-tuple-element.28, bf16[128,1024]{1,0:T(8,128)(2,1)} %collective-permute-done.9, bf16[1024,1024]{1,0:T(8,128)(2,1)S(1)} %get-tuple-element.26), kind=kOutput, calls=%fused_computation.117 | convolution fusion | flops 269221888 | bytes 3145728 | tf_op jit(solution)/shard_map/dot_general | solution.py:22
  28.0 1.0 convert_add_fusion
  29.0 0.7 collective-permute-start.3
  29.7 0.4 fusion.24
  30.2 1.0 collective-permute-start.13
  31.1 0.5 multiply_convert_fusion.5
  31.7 0.4 fusion.58
  32.1 1.8 %collective-permute-start.12 = (bf16[128,1024]{1,0:T(8,128)(2,1)S(1)}, bf16[128,1024]{1,0:T(8,128)(2,1)S(1)}, u32[]{:S(2)}, u32[]{:S(2)}) collective-permute-start(bf16[128,1024]{1,0:T(8,128)(2,1)S(1)} %multiply_convert_fusion.5), channel_id=1, source_target_pairs={{0,128},{16,144},{32,160},{48,176},{64,192},{80,208},{96,224},{112... | collective-permute-start | bytes 786440 | tf_op jit(solution)/shard_map/ppermute | solution.py:18
  33.9 0.4 fusion.22
  34.4 0.7 collective-permute-start.15
  35.1 4.3 %collective-permute-start.4 = (f32[128,256]{1,0:T(8,128)S(1)}, f32[128,256]{1,0:T(8,128)S(1)}, u32[]{:S(2)}, u32[]{:S(2)}) collective-permute-start(f32[128,256]{1,0:T(8,128)S(1)} %constant_dynamic-slice_fusion.14), channel_id=1, source_target_pairs={{0,64},{16,80},{32,96},{48,112},{64,0},{80,16},{96,32},{112,48},{1... | collective-permute-start | bytes 393224 | tf_op jit(solution)/shard_map/ppermute | solution.py:18
  39.5 1.1 collective-permute-done.13
  40.6 0.5 multiply_convert_fusion.4
  41.1 1.7 %collective-permute-start.14 = (bf16[128,1024]{1,0:T(8,128)(2,1)S(1)}, bf16[128,1024]{1,0:T(8,128)(2,1)S(1)}, u32[]{:S(2)}, u32[]{:S(2)}) collective-permute-start(bf16[128,1024]{1,0:T(8,128)(2,1)S(1)} %multiply_convert_fusion.4), channel_id=1, source_target_pairs={{0,128},{16,144},{32,160},{48,176},{64,192},{80,208},{96,224},{112... | collective-permute-start | bytes 786440 | tf_op jit(solution)/shard_map/ppermute | solution.py:18
  42.8 0.4 fusion.56
  43.3 0.5 collective-permute-done.10
  43.8 0.5 divide_multiply_fusion.5
  44.3 0.4 fusion.20
  44.9 0.8 collective-permute-start.5
  46.2 0.5 multiply_convert_fusion.3
  46.7 11.5 %collective-permute-done.12 = bf16[128,1024]{1,0:T(8,128)(2,1)S(1)} collective-permute-done((bf16[128,1024]{1,0:T(8,128)(2,1)S(1)}, bf16[128,1024]{1,0:T(8,128)(2,1)S(1)}, u32[]{:S(2)}, u32[]{:S(2)}) %collective-permute-start.12) | collective-permute-done | bytes 262176 | tf_op jit(solution)/shard_map/ppermute | solution.py:18
  58.2 0.5 divide_multiply_fusion.4
  58.7 0.4 fusion.54
  59.2 11.6 %collective-permute-done.5 = bf16[128,256]{1,0:T(8,128)(2,1)S(1)} collective-permute-done((bf16[128,256]{1,0:T(8,128)(2,1)S(1)}, bf16[128,256]{1,0:T(8,128)(2,1)S(1)}, u32[]{:S(2)}, u32[]{:S(2)}) %collective-permute-start.5) | collective-permute-done | bytes 65568 | tf_op jit(solution)/shard_map/ppermute | solution.py:18
  70.9 0.4 fusion.18
  71.4 0.7 collective-permute-start.19
  72.1 7.5 %collective-permute-done.6 = bf16[128,256]{1,0:T(8,128)(2,1)S(1)} collective-permute-done((bf16[128,256]{1,0:T(8,128)(2,1)S(1)}, bf16[128,256]{1,0:T(8,128)(2,1)S(1)}, u32[]{:S(2)}, u32[]{:S(2)}) %collective-permute-start.6) | collective-permute-done | bytes 65568 | tf_op jit(solution)/shard_map/ppermute | solution.py:18
  79.9 0.5 multiply_convert_fusion.2
  80.5 0.4 fusion.52
  81.0 0.5 divide_multiply_fusion.3
  81.5 0.4 fusion.16
  82.0 1.3 %collective-permute-start.21 = (bf16[128,1024]{1,0:T(8,128)(2,1)S(1)}, bf16[128,1024]{1,0:T(8,128)(2,1)S(1)}, u32[]{:S(2)}, u32[]{:S(2)}) collective-permute-start(bf16[128,1024]{1,0:T(8,128)(2,1)S(1)} %slice.50), channel_id=1, source_target_pairs={{0,16},{16,0},{32,48},{48,32},{64,80},{80,64},{96,112},{112,96},{1... | collective-permute-start | bytes 786440 | tf_op jit(solution)/shard_map/ppermute | solution.py:18
  83.3 0.9 collective-permute-done.7
  84.2 0.5 collective-permute-start.8
  84.8 0.5 multiply_convert_fusion.1
  85.3 1.6 %collective-permute-start.20 = (bf16[128,1024]{1,0:T(8,128)(2,1)S(1)}, bf16[128,1024]{1,0:T(8,128)(2,1)S(1)}, u32[]{:S(2)}, u32[]{:S(2)}) collective-permute-start(bf16[128,1024]{1,0:T(8,128)(2,1)S(1)} %multiply_convert_fusion.1), channel_id=1, source_target_pairs={{0,128},{16,144},{32,160},{48,176},{64,192},{80,208},{96,224},{112... | collective-permute-start | bytes 786440 | tf_op jit(solution)/shard_map/ppermute | solution.py:18
  87.4 0.5 divide_multiply_fusion.2
  87.9 0.5 fusion.14
  88.7 0.9 collective-permute-done.21
  89.6 0.5 multiply_convert_fusion
  90.1 1.4 %collective-permute-start.22 = (bf16[128,1024]{1,0:T(8,128)(2,1)S(1)}, bf16[128,1024]{1,0:T(8,128)(2,1)S(1)}, u32[]{:S(2)}, u32[]{:S(2)}) collective-permute-start(bf16[128,1024]{1,0:T(8,128)(2,1)S(1)} %multiply_convert_fusion), channel_id=1, source_target_pairs={{0,128},{16,144},{32,160},{48,176},{64,192},{80,208},{96,224},{112... | collective-permute-start | bytes 786440 | tf_op jit(solution)/shard_map/ppermute | solution.py:18
  91.9 13.6 %collective-permute-done.18 = bf16[128,1024]{1,0:T(8,128)(2,1)S(1)} collective-permute-done((bf16[128,1024]{1,0:T(8,128)(2,1)S(1)}, bf16[128,1024]{1,0:T(8,128)(2,1)S(1)}, u32[]{:S(2)}, u32[]{:S(2)}) %collective-permute-start.18) | collective-permute-done | bytes 262176 | tf_op jit(solution)/shard_map/ppermute | solution.py:18
  105.6 0.5 divide_multiply_fusion.1
  106.1 0.5 multiply_convert_fusion.7
  106.7 0.5 fusion.46
  109.8 12.6 %collective-permute-done.24 = bf16[64,1024]{1,0:T(8,128)(2,1)S(1)} collective-permute-done((bf16[64,1024]{1,0:T(8,128)(2,1)S(1)}, bf16[64,1024]{1,0:T(8,128)(2,1)S(1)}, u32[]{:S(2)}, u32[]{:S(2)}) %collective-permute-start.24) | collective-permute-done | bytes 131104 | tf_op jit(solution)/shard_map/ppermute | solution.py:18
  122.4 0.5 fusion.106
  123.2 0.5 divide_multiply_fusion
  123.8 0.5 fusion.128
  124.3 1.3 %copy-done.2 = bf16[1024,1024]{1,0:T(8,128)(2,1)} copy-done((bf16[1024,1024]{1,0:T(8,128)(2,1)}, bf16[1024,1024]{1,0:T(8,128)(2,1)S(1)}, u32[]{:S(2)}) %copy-start.2) | copy-done | bytes 2097176
  125.7 0.7 fusion.165
  (76 shorter events, 7.2 us)
Async XLA Ops:
  0.0 107.3 %copy-start = (bf16[256,1024]{1,0:T(8,128)(2,1)S(1)}, bf16[256,1024]{1,0:T(8,128)(2,1)}, u32[]{:S(2)}) copy-start(bf16[256,1024]{1,0:T(8,128)(2,1)} %param.7) | copy-start | bytes 1572868
  1.0 12.1 %collective-permute-start = (bf16[64,1024]{1,0:T(8,128)(2,1)S(1)}, bf16[64,1024]{1,0:T(8,128)(2,1)}, u32[]{:S(2)}, u32[]{:S(2)}) collective-permute-start(bf16[64,1024]{1,0:T(8,128)(2,1)S(1)} %slice.39), channel_id=1, source_target_pairs={{0,16},{16,0},{32,48},{48,32},{64,80},{80,64},{96,112},{112,96},{1... | collective-permute-start | bytes 393224 | tf_op jit(solution)/shard_map/ppermute | solution.py:18
  5.6 4.8 %copy-start.3 = (f32[1024,256]{1,0:T(8,128)}, f32[1024,256]{1,0:T(8,128)S(1)}, u32[]{:S(2)}) copy-start(f32[1024,256]{1,0:T(8,128)S(1)} %fusion.232) | copy-start | bytes 3145732
  6.4 21.2 %collective-permute-start.2 = (bf16[512,256]{1,0:T(8,128)(2,1)}, bf16[512,256]{1,0:T(8,128)(2,1)}, u32[]{:S(2)}, u32[]{:S(2)}) collective-permute-start(bf16[512,256]{1,0:T(8,128)(2,1)} %dynamic-slice_convert_fusion), channel_id=1, source_target_pairs={{0,48},{16,32},{32,16},{48,0},{64,112},{80,96},{96,80},{112,64},{1... | collective-permute-start | bytes 786440 | tf_op jit(solution)/shard_map/ppermute | solution.py:18
  10.0 15.3 %collective-permute-start.9 = (bf16[128,1024]{1,0:T(8,128)(2,1)}, bf16[128,1024]{1,0:T(8,128)(2,1)}, u32[]{:S(2)}, u32[]{:S(2)}) collective-permute-start(bf16[128,1024]{1,0:T(8,128)(2,1)} %slice.42), channel_id=1, source_target_pairs={{0,16},{16,0},{32,48},{48,32},{64,80},{80,64},{96,112},{112,96},{1... | collective-permute-start | bytes 786440 | tf_op jit(solution)/shard_map/ppermute | solution.py:18
  13.1 4.7 %copy-start.1 = (bf16[1024,1024]{1,0:T(8,128)(2,1)S(1)}, bf16[1024,1024]{1,0:T(8,128)(2,1)}, u32[]{:S(2)}) copy-start(bf16[1024,1024]{1,0:T(8,128)(2,1)} %t_ref.1) | copy-start | bytes 6291460
  13.1 14.0 %slice-start = ((s8[8388608]{0:T(1024)(128)(4,1)}), s8[4194304]{0:T(1024)(128)(4,1)S(1)}, s32[]{:S(2)}) async-start(s8[8388608]{0:T(1024)(128)(4,1)} %bitcast.172), calls=%async_computation | async-start | bytes 8388608
  14.7 8.4 %collective-permute-start.1 = (bf16[64,1024]{1,0:T(8,128)(2,1)S(1)}, bf16[64,1024]{1,0:T(8,128)(2,1)S(1)}, u32[]{:S(2)}, u32[]{:S(2)}) collective-permute-start(bf16[64,1024]{1,0:T(8,128)(2,1)S(1)} %multiply_convert_fusion.8), channel_id=1, source_target_pairs={{0,128},{16,144},{32,160},{48,176},{64,192},{80,208},{96,224},{112... | collective-permute-start | bytes 393224 | tf_op jit(solution)/shard_map/ppermute | solution.py:18
  21.9 5.2 %slice-start.1 = ((s8[8388608]{0:T(1024)(128)(4,1)}), s8[4194304]{0:T(1024)(128)(4,1)S(1)}, s32[]{:S(2)}) async-start(s8[8388608]{0:T(1024)(128)(4,1)} %bitcast.172), calls=%async_computation.1 | async-start | bytes 8388608
  21.9 9.2 %collective-permute-start.11 = (bf16[128,1024]{1,0:T(8,128)(2,1)S(1)}, bf16[128,1024]{1,0:T(8,128)(2,1)S(1)}, u32[]{:S(2)}, u32[]{:S(2)}) collective-permute-start(bf16[128,1024]{1,0:T(8,128)(2,1)S(1)} %slice.43), channel_id=1, source_target_pairs={{0,16},{16,0},{32,48},{48,32},{64,80},{80,64},{96,112},{112,96},{1... | collective-permute-start | bytes 786440 | tf_op jit(solution)/shard_map/ppermute | solution.py:18
  26.7 1.2 copy-start.4
  26.8 17.0 %collective-permute-start.10 = (bf16[128,1024]{1,0:T(8,128)(2,1)S(1)}, bf16[128,1024]{1,0:T(8,128)(2,1)S(1)}, u32[]{:S(2)}, u32[]{:S(2)}) collective-permute-start(bf16[128,1024]{1,0:T(8,128)(2,1)S(1)} %multiply_convert_fusion.6), channel_id=1, source_target_pairs={{0,128},{16,144},{32,160},{48,176},{64,192},{80,208},{96,224},{112... | collective-permute-start | bytes 786440 | tf_op jit(solution)/shard_map/ppermute | solution.py:18
  29.0 6.1 %collective-permute-start.3 = (f32[256,256]{1,0:T(8,128)S(1)}, f32[256,256]{1,0:T(8,128)S(1)}, u32[]{:S(2)}, u32[]{:S(2)}) collective-permute-start(f32[256,256]{1,0:T(8,128)S(1)} %constant_dynamic-slice_fusion.15), channel_id=1, source_target_pairs={{0,16},{16,0},{32,48},{48,32},{64,80},{80,64},{96,112},{112,96},{1... | collective-permute-start | bytes 786440 | tf_op jit(solution)/shard_map/ppermute | solution.py:18
  30.2 10.4 %collective-permute-start.13 = (bf16[128,1024]{1,0:T(8,128)(2,1)S(1)}, bf16[128,1024]{1,0:T(8,128)(2,1)S(1)}, u32[]{:S(2)}, u32[]{:S(2)}) collective-permute-start(bf16[128,1024]{1,0:T(8,128)(2,1)S(1)} %slice.46), channel_id=1, source_target_pairs={{0,16},{16,0},{32,48},{48,32},{64,80},{80,64},{96,112},{112,96},{1... | collective-permute-start | bytes 786440 | tf_op jit(solution)/shard_map/ppermute | solution.py:18
  32.1 26.1 %collective-permute-start.12 = (bf16[128,1024]{1,0:T(8,128)(2,1)S(1)}, bf16[128,1024]{1,0:T(8,128)(2,1)S(1)}, u32[]{:S(2)}, u32[]{:S(2)}) collective-permute-start(bf16[128,1024]{1,0:T(8,128)(2,1)S(1)} %multiply_convert_fusion.5), channel_id=1, source_target_pairs={{0,128},{16,144},{32,160},{48,176},{64,192},{80,208},{96,224},{112... | collective-permute-start | bytes 786440 | tf_op jit(solution)/shard_map/ppermute | solution.py:18
  34.4 11.8 %collective-permute-start.15 = (bf16[128,1024]{1,0:T(8,128)(2,1)S(1)}, bf16[128,1024]{1,0:T(8,128)(2,1)S(1)}, u32[]{:S(2)}, u32[]{:S(2)}) collective-permute-start(bf16[128,1024]{1,0:T(8,128)(2,1)S(1)} %slice.47), channel_id=1, source_target_pairs={{0,16},{16,0},{32,48},{48,32},{64,80},{80,64},{96,112},{112,96},{1... | collective-permute-start | bytes 786440 | tf_op jit(solution)/shard_map/ppermute | solution.py:18
  35.1 9.7 %collective-permute-start.4 = (f32[128,256]{1,0:T(8,128)S(1)}, f32[128,256]{1,0:T(8,128)S(1)}, u32[]{:S(2)}, u32[]{:S(2)}) collective-permute-start(f32[128,256]{1,0:T(8,128)S(1)} %constant_dynamic-slice_fusion.14), channel_id=1, source_target_pairs={{0,64},{16,80},{32,96},{48,112},{64,0},{80,16},{96,32},{112,48},{1... | collective-permute-start | bytes 393224 | tf_op jit(solution)/shard_map/ppermute | solution.py:18
  41.1 39.9 %collective-permute-start.14 = (bf16[128,1024]{1,0:T(8,128)(2,1)S(1)}, bf16[128,1024]{1,0:T(8,128)(2,1)S(1)}, u32[]{:S(2)}, u32[]{:S(2)}) collective-permute-start(bf16[128,1024]{1,0:T(8,128)(2,1)S(1)} %multiply_convert_fusion.4), channel_id=1, source_target_pairs={{0,128},{16,144},{32,160},{48,176},{64,192},{80,208},{96,224},{112... | collective-permute-start | bytes 786440 | tf_op jit(solution)/shard_map/ppermute | solution.py:18
  44.8 35.1 %collective-permute-start.17 = (bf16[128,1024]{1,0:T(8,128)(2,1)S(1)}, bf16[128,1024]{1,0:T(8,128)(2,1)S(1)}, u32[]{:S(2)}, u32[]{:S(2)}) collective-permute-start(bf16[128,1024]{1,0:T(8,128)(2,1)S(1)} %slice.48), channel_id=1, source_target_pairs={{0,16},{16,0},{32,48},{48,32},{64,80},{80,64},{96,112},{112,96},{1... | collective-permute-start | bytes 786440 | tf_op jit(solution)/shard_map/ppermute | solution.py:18
  44.9 25.9 %collective-permute-start.5 = (bf16[128,256]{1,0:T(8,128)(2,1)S(1)}, bf16[128,256]{1,0:T(8,128)(2,1)S(1)}, u32[]{:S(2)}, u32[]{:S(2)}) collective-permute-start(bf16[128,256]{1,0:T(8,128)(2,1)S(1)} %convert_element_type.72), channel_id=1, source_target_pairs={{0,128},{16,144},{32,160},{48,176},{64,192},{80,208},{96,224},{112... | collective-permute-start | bytes 196616 | tf_op jit(solution)/shard_map/ppermute | solution.py:18
  59.1 28.2 %collective-permute-start.16 = (bf16[128,1024]{1,0:T(8,128)(2,1)S(1)}, bf16[128,1024]{1,0:T(8,128)(2,1)S(1)}, u32[]{:S(2)}, u32[]{:S(2)}) collective-permute-start(bf16[128,1024]{1,0:T(8,128)(2,1)S(1)} %multiply_convert_fusion.3), channel_id=1, source_target_pairs={{0,128},{16,144},{32,160},{48,176},{64,192},{80,208},{96,224},{112... | collective-permute-start | bytes 786440 | tf_op jit(solution)/shard_map/ppermute | solution.py:18
  70.8 8.7 %collective-permute-start.6 = (bf16[128,256]{1,0:T(8,128)(2,1)S(1)}, bf16[128,256]{1,0:T(8,128)(2,1)S(1)}, u32[]{:S(2)}, u32[]{:S(2)}) collective-permute-start(bf16[128,256]{1,0:T(8,128)(2,1)S(1)} %add_convert_fusion.9), channel_id=1, source_target_pairs={{0,64},{16,80},{32,96},{48,112},{64,0},{80,16},{96,32},{112,48},{1... | collective-permute-start | bytes 196616 | tf_op jit(solution)/shard_map/ppermute | solution.py:18
  71.4 13.4 %collective-permute-start.19 = (bf16[128,1024]{1,0:T(8,128)(2,1)S(1)}, bf16[128,1024]{1,0:T(8,128)(2,1)S(1)}, u32[]{:S(2)}, u32[]{:S(2)}) collective-permute-start(bf16[128,1024]{1,0:T(8,128)(2,1)S(1)} %slice.49), channel_id=1, source_target_pairs={{0,16},{16,0},{32,48},{48,32},{64,80},{80,64},{96,112},{112,96},{1... | collective-permute-start | bytes 786440 | tf_op jit(solution)/shard_map/ppermute | solution.py:18
  79.6 4.7 %collective-permute-start.7 = (bf16[256,256]{1,0:T(8,128)(2,1)S(1)}, bf16[256,256]{1,0:T(8,128)(2,1)S(1)}, u32[]{:S(2)}, u32[]{:S(2)}) collective-permute-start(bf16[256,256]{1,0:T(8,128)(2,1)S(1)} %pad_maximum_fusion.2), channel_id=1, source_target_pairs={{0,16},{16,0},{32,48},{48,32},{64,80},{80,64},{96,112},{112,96},{1... | collective-permute-start | bytes 393224 | tf_op jit(solution)/shard_map/ppermute | solution.py:18
  80.4 25.1 %collective-permute-start.18 = (bf16[128,1024]{1,0:T(8,128)(2,1)S(1)}, bf16[128,1024]{1,0:T(8,128)(2,1)S(1)}, u32[]{:S(2)}, u32[]{:S(2)}) collective-permute-start(bf16[128,1024]{1,0:T(8,128)(2,1)S(1)} %multiply_convert_fusion.2), channel_id=1, source_target_pairs={{0,128},{16,144},{32,160},{48,176},{64,192},{80,208},{96,224},{112... | collective-permute-start | bytes 786440 | tf_op jit(solution)/shard_map/ppermute | solution.py:18
  82.0 7.6 %collective-permute-start.21 = (bf16[128,1024]{1,0:T(8,128)(2,1)S(1)}, bf16[128,1024]{1,0:T(8,128)(2,1)S(1)}, u32[]{:S(2)}, u32[]{:S(2)}) collective-permute-start(bf16[128,1024]{1,0:T(8,128)(2,1)S(1)} %slice.50), channel_id=1, source_target_pairs={{0,16},{16,0},{32,48},{48,32},{64,80},{80,64},{96,112},{112,96},{1... | collective-permute-start | bytes 786440 | tf_op jit(solution)/shard_map/ppermute | solution.py:18
  84.2 23.0 %collective-permute-start.8 = (bf16[512,256]{1,0:T(8,128)(2,1)S(1)}, bf16[512,256]{1,0:T(8,128)(2,1)S(1)}, u32[]{:S(2)}, u32[]{:S(2)}) collective-permute-start(bf16[512,256]{1,0:T(8,128)(2,1)S(1)} %pad_maximum_fusion.1), channel_id=1, source_target_pairs={{0,48},{16,32},{32,16},{48,0},{64,112},{80,96},{96,80},{112,64},{1... | collective-permute-start | bytes 786440 | tf_op jit(solution)/shard_map/ppermute | solution.py:18
  85.3 37.9 %collective-permute-start.20 = (bf16[128,1024]{1,0:T(8,128)(2,1)S(1)}, bf16[128,1024]{1,0:T(8,128)(2,1)S(1)}, u32[]{:S(2)}, u32[]{:S(2)}) collective-permute-start(bf16[128,1024]{1,0:T(8,128)(2,1)S(1)} %multiply_convert_fusion.1), channel_id=1, source_target_pairs={{0,128},{16,144},{32,160},{48,176},{64,192},{80,208},{96,224},{112... | collective-permute-start | bytes 786440 | tf_op jit(solution)/shard_map/ppermute | solution.py:18
  88.4 17.7 %collective-permute-start.23 = (bf16[64,1024]{1,0:T(8,128)(2,1)S(1)}, bf16[64,1024]{1,0:T(8,128)(2,1)S(1)}, u32[]{:S(2)}, u32[]{:S(2)}) collective-permute-start(bf16[64,1024]{1,0:T(8,128)(2,1)S(1)} %slice.51), channel_id=1, source_target_pairs={{0,16},{16,0},{32,48},{48,32},{64,80},{80,64},{96,112},{112,96},{1... | collective-permute-start | bytes 393224 | tf_op jit(solution)/shard_map/ppermute | solution.py:18
  90.1 33.7 %collective-permute-start.22 = (bf16[128,1024]{1,0:T(8,128)(2,1)S(1)}, bf16[128,1024]{1,0:T(8,128)(2,1)S(1)}, u32[]{:S(2)}, u32[]{:S(2)}) collective-permute-start(bf16[128,1024]{1,0:T(8,128)(2,1)S(1)} %multiply_convert_fusion), channel_id=1, source_target_pairs={{0,128},{16,144},{32,160},{48,176},{64,192},{80,208},{96,224},{112... | collective-permute-start | bytes 786440 | tf_op jit(solution)/shard_map/ppermute | solution.py:18
  106.6 15.8 %collective-permute-start.24 = (bf16[64,1024]{1,0:T(8,128)(2,1)S(1)}, bf16[64,1024]{1,0:T(8,128)(2,1)S(1)}, u32[]{:S(2)}, u32[]{:S(2)}) collective-permute-start(bf16[64,1024]{1,0:T(8,128)(2,1)S(1)} %multiply_convert_fusion.7), channel_id=1, source_target_pairs={{0,128},{16,144},{32,160},{48,176},{64,192},{80,208},{96,224},{112... | collective-permute-start | bytes 393224 | tf_op jit(solution)/shard_map/ppermute | solution.py:18
  124.3 1.3 %copy-start.2 = (bf16[1024,1024]{1,0:T(8,128)(2,1)}, bf16[1024,1024]{1,0:T(8,128)(2,1)S(1)}, u32[]{:S(2)}) copy-start(bf16[1024,1024]{1,0:T(8,128)(2,1)S(1)} %fusion.128) | copy-start | bytes 6291460

commit v3 on v2

--- a/solution.py
+++ b/solution.py
@@ -5,11 +5,13 @@
 from jax.experimental.pallas import tpu as pltpu
 from jax.sharding import PartitionSpec as P
 
-ROWS = (64, 128, 128, 128, 128, 128, 128, 128, 64)
+ROWS = (64, 64, 128, 128, 128, 128, 160, 160, 64)
 BOUNDS = tuple((sum(ROWS[:i]), sum(ROWS[: i + 1])) for i in range(len(ROWS)))
 LAST = len(ROWS) - 1
 PIECES = 8
 OPENING = 2
+PARTS = 4
+LIMIT = 54
 FAST = 2
 
 
@@ -24,39 +26,48 @@
 
 def opening(tokens, weights, sizes):
     width = tokens.shape[1]
-    rows = sum(sizes)
+    count = len(sizes)
+    piece = width // PARTS
 
     def body(t_ref, w_ref, *refs):
-        *own_refs, other_ref, rows_ref, own_w_ref, sems = refs
-        copies = [
-            pltpu.make_async_copy(t_ref.at[pl.ds(0, rows)], rows_ref, sems.at[0]),
-            pltpu.make_async_copy(w_ref.at[0, pl.ds(0, width)], own_w_ref, sems.at[1]),
-            pltpu.make_async_copy(w_ref.at[0, pl.ds(width, width)], other_ref, sems.at[2]),
-        ]
+        own_refs, chunk_refs = refs[:count], refs[count : 2 * count - 1]
+        other_ref, first_ref, own_w_ref, sems = refs[2 * count - 1 :]
+        chunk_refs = (first_ref, *chunk_refs)
+        loads = []
+        start = 0
+        for ref, size in zip(chunk_refs, sizes):
+            loads.append((t_ref.at[pl.ds(start, size)], ref))
+            start += size
+        for offset, ref in ((0, own_w_ref), (width, other_ref)):
+            for k in range(PARTS):
+                loads.append(
+                    (w_ref.at[0, pl.ds(offset + k * piece, piece)], ref.at[pl.ds(k * piece, piece)])
+                )
+        copies = [pltpu.make_async_copy(*load, sems.at[i]) for i, load in enumerate(loads)]
         for copy in copies:
             copy.start()
-        copies[0].wait()
-        copies[1].wait()
-        start = 0
-        for own_ref, size in zip(own_refs, sizes):
-            own_ref[...] = product(rows_ref[pl.ds(start, size)], own_w_ref[...])
-            start += size
-        copies[2].wait()
+        for copy in copies[: count + PARTS]:
+            copy.wait()
+        for own_ref, ref in zip(own_refs, chunk_refs):
+            own_ref[...] = product(ref[...], own_w_ref[...])
+        for copy in copies[count + PARTS :]:
+            copy.wait()
 
     return pl.pallas_call(
         body,
         out_shape=(
             *(pltpu.VMEM((size, width), jnp.float32) for size in sizes),
+            *(pltpu.VMEM((size, width), tokens.dtype) for size in sizes[1:]),
             pltpu.VMEM((width, width), weights.dtype),
         ),
         in_specs=[pl.BlockSpec(memory_space=pl.ANY), pl.BlockSpec(memory_space=pl.ANY)],
-        out_specs=tuple(pl.BlockSpec(memory_space=pltpu.VMEM) for _ in range(len(sizes) + 1)),
+        out_specs=tuple(pl.BlockSpec(memory_space=pltpu.VMEM) for _ in range(2 * count)),
         scratch_shapes=[
-            pltpu.VMEM((rows, width), tokens.dtype),
+            pltpu.VMEM((sizes[0], width), tokens.dtype),
             pltpu.VMEM((width, width), weights.dtype),
-            pltpu.SemaphoreType.DMA((3,)),
+            pltpu.SemaphoreType.DMA((count + 2 * PARTS,)),
         ],
-        compiler_params=pltpu.CompilerParams(vmem_limit_bytes=56 << 20),
+        compiler_params=pltpu.CompilerParams(vmem_limit_bytes=LIMIT << 20),
         name="opening",
     )(tokens, weights)
 
@@ -86,18 +97,17 @@
         source, done = lax.optimization_barrier((tokens, done))
         return cut(source, k), done
 
-    rows, partner, own, state, received = [cut(tokens, 0)], [], [], [], []
+    rows, partner, state, received = [cut(tokens, 0)], [], [], []
+    made = opening(tokens, pair_weights, ROWS[:OPENING])
+    own = list(made[:OPENING])
+    rows += made[OPENING:-1]
+    fast_other = made[-1]
     for k in chunks:
-        if k == 1:
-            chunk, rank_up = after(rank_up, k)
-            rows.append(chunk)
-        elif k > 1:
+        if k >= OPENING:
             chunk, partner[k - 2] = after(partner[k - 2], k)
             rows.append(chunk)
         partner.append(exchanged(rows[k], 1))
-        if k == 0:
-            *own, fast_other = opening(tokens, pair_weights, ROWS[:OPENING])
-        elif k >= OPENING:
+        if k >= OPENING:
             own.append(lax.optimization_barrier(product(rows[k], w_own)))
     for k in chunks:
         left = fast_other if k < FAST else w_other

time: 127 us -> 138 us (1.087)
  starting transfers between devices: 26.7 us -> 35.9 us
  matrix products: 27.5 us -> 30.1 us
  waiting for transfers between devices: 60.8 us -> 62.5 us
    ppermute x25, starting transfers between devices: 26.7 us -> 35.9 us  [exchanged(): return lax.ppermute(block, 'feat', [(i, i ^ stride) for i in range(count)])]
    dot_general x44, matrix products: 27.5 us -> 30.1 us  [product(): return jnp.dot(left, right, preferred_element_type=jnp.float32)]
    ppermute x25, waiting for transfers between devices: 60.8 us -> 62.5 us  [exchanged(): return lax.ppermute(block, 'feat', [(i, i ^ stride) for i in range(count)])]
  transfers between devices with their start and end apart: 25 -> 25, of which waited for: 10 -> 11; matrix products, arithmetic and copies ran while one was open for 25% -> 23% of each run, Pallas kernels for 2% -> 2%
where the time goes in v3:
time: 138 us
  waiting for transfers between devices  62.5 us (45%)
  starting transfers between devices  35.9 us (26%)
  matrix products  30.1 us (22%)
  local copies, waits for them, and re-layouts  4.47 us (3%)
  Pallas kernels  2.59 us (2%)
    ppermute x25, waiting for transfers between devices, exchanged(): return lax.ppermute(block, 'feat', [(i, i ^ stride) for i in range(count)])  62.5 us
    ppermute x25, starting transfers between devices, exchanged(): return lax.ppermute(block, 'feat', [(i, i ^ stride) for i in range(count)])  35.9 us
    dot_general x44, matrix products, product(): return jnp.dot(left, right, preferred_element_type=jnp.float32)  30.1 us
  transfers between devices with their start and end apart: 25, of which 11 were waited for; matrix products, arithmetic and copies ran while one was open for 23% of the time, Pallas kernels for 2%

profile of v3, /device:TPU:1, one launch (start us, length us, event | category | flops | bytes accessed | tf_op | source)
XLA Modules:
  0.0 137.5 jit_solution(16822136028794950954)
XLA Ops:
  0.0 1.6 %slice.36 = bf16[64,1024]{1,0:T(8,128)(2,1)} slice(bf16[1024,1024]{1,0:T(8,128)(2,1)} %t_ref.1), slice={[0:64], [0:1024]} | slice | bytes 262144 | tf_op jit(solution)/shard_map/slice | solution.py:94
  1.6 2.1 %collective-permute-start = (bf16[64,1024]{1,0:T(8,128)(2,1)}, bf16[64,1024]{1,0:T(8,128)(2,1)}, u32[]{:S(2)}, u32[]{:S(2)}) collective-permute-start(bf16[64,1024]{1,0:T(8,128)(2,1)} %slice.36), channel_id=1, source_target_pairs={{0,16},{16,0},{32,48},{48,32},{64,80},{80,64},{96,112},{112,96},{1... | collective-permute-start | bytes 393224 | tf_op jit(solution)/shard_map/ppermute | solution.py:20
  3.7 2.4 %fusion.222 = f32[1024,256]{1,0:T(8,128)S(1)} fusion(bf16[1024,1024]{1,0:T(8,128)(2,1)} %t_ref.1, bf16[1024,256]{1,0:T(8,128)(2,1)} %param.6), kind=kOutput, calls=%fused_computation.199 | convolution fusion | flops 536870912 | bytes 3670016 | tf_op jit(solution)/shard_map/dot_general | solution.py:24
  6.1 0.8 dynamic-slice_convert_fusion
  7.2 1.9 %collective-permute-start.2 = (bf16[512,256]{1,0:T(8,128)(2,1)}, bf16[512,256]{1,0:T(8,128)(2,1)S(1)}, u32[]{:S(2)}, u32[]{:S(2)}) collective-permute-start(bf16[512,256]{1,0:T(8,128)(2,1)} %dynamic-slice_convert_fusion), channel_id=1, source_target_pairs={{0,48},{16,32},{32,16},{48,0},{64,112},{80,96},{96,80},{112,64},{1... | collective-permute-start | bytes 786440 | tf_op jit(solution)/shard_map/ppermute | solution.py:20
  9.1 2.6 %opening.1 = (f32[64,1024]{1,0:T(8,128)S(1)}, f32[64,1024]{1,0:T(8,128)S(1)}, bf16[64,1024]{1,0:T(8,128)(2,1)S(1)}, bf16[1024,1024]{1,0:T(8,128)(2,1)S(1)}) custom-call(bf16[1024,1024]{1,0:T(8,128)(2,1)} %t_ref.1, bf16[2,2048,1024]{2,1,0:T(8,128)(2,1)} %w_ref.1), custom_call_target="tpu_custom_call" | custom-call | tf_op jit(solution)/shard_map/opening/pallas_call | solution.py:56
  11.7 0.5 collective-permute-start.9
  12.2 1.4 %multiply_convert_fusion.8 = bf16[64,1024]{1,0:T(8,128)(2,1)S(1)} fusion(f32[64,1024]{1,0:T(8,128)S(1)} %get-tuple-element.23, bf16[64,1024]{1,0:T(8,128)(2,1)} %collective-permute-done, bf16[1024,1024]{1,0:T(8,128)(2,1)S(1)} %get-tuple-element.25), kind=kOutput, calls=%fused_computation.131 | convolution fusion | flops 134610944 | bytes 2621440 | tf_op jit(solution)/shard_map/dot_general | solution.py:24
  13.6 2.2 %fusion.62 = f32[64,1024]{1,0:T(8,128)S(1)} fusion(bf16[64,1024]{1,0:T(8,128)(2,1)S(1)} %multiply_convert_fusion.8, bf16[2,2048,1024]{2,1,0:T(8,128)(2,1)} %w_ref.1), kind=kOutput, calls=%fused_computation.62 | convolution fusion | flops 134217728 | bytes 2490368 | tf_op jit(solution)/shard_map/dot_general | solution.py:24
  15.8 3.1 %collective-permute-start.1 = (bf16[64,1024]{1,0:T(8,128)(2,1)S(1)}, bf16[64,1024]{1,0:T(8,128)(2,1)S(1)}, u32[]{:S(2)}, u32[]{:S(2)}) collective-permute-start(bf16[64,1024]{1,0:T(8,128)(2,1)S(1)} %multiply_convert_fusion.8), channel_id=1, source_target_pairs={{0,128},{16,144},{32,160},{48,176},{64,192},{80,208},{96,224},{112... | collective-permute-start | bytes 393224 | tf_op jit(solution)/shard_map/ppermute | solution.py:20
  18.9 1.6 %multiply_convert_fusion.7 = bf16[64,1024]{1,0:T(8,128)(2,1)S(1)} fusion(f32[64,1024]{1,0:T(8,128)S(1)} %get-tuple-element.26, bf16[64,1024]{1,0:T(8,128)(2,1)} %collective-permute-done.9, bf16[1024,1024]{1,0:T(8,128)(2,1)S(1)} %get-tuple-element.25), kind=kOutput, calls=%fused_computation.127 | convolution fusion | flops 134610944 | bytes 2621440 | tf_op jit(solution)/shard_map/dot_general | solution.py:24
  20.5 2.1 %fusion.60 = f32[64,1024]{1,0:T(8,128)S(1)} fusion(bf16[64,1024]{1,0:T(8,128)(2,1)S(1)} %multiply_convert_fusion.7, bf16[2,2048,1024]{2,1,0:T(8,128)(2,1)} %w_ref.1), kind=kOutput, calls=%fused_computation.60 | convolution fusion | flops 134217728 | bytes 2490368 | tf_op jit(solution)/shard_map/dot_general | solution.py:24
  22.7 2.2 %fusion.26 = f32[128,1024]{1,0:T(8,128)S(1)} fusion(bf16[2,2048,1024]{2,1,0:T(8,128)(2,1)} %w_ref.1, bf16[1024,1024]{1,0:T(8,128)(2,1)S(1)} %copy-done.1), kind=kOutput, calls=%fused_computation.26 | convolution fusion | flops 268435456 | bytes 2883584 | tf_op jit(solution)/shard_map/dot_general | solution.py:24
  24.9 1.2 collective-permute-start.11
  26.1 0.5 collective-permute-start.13
  26.6 2.0 %fusion.24 = f32[128,1024]{1,0:T(8,128)S(1)} fusion(bf16[2,2048,1024]{2,1,0:T(8,128)(2,1)} %w_ref.1, bf16[1024,1024]{1,0:T(8,128)(2,1)S(1)} %copy-done.1), kind=kOutput, calls=%fused_computation.24 | convolution fusion | flops 268435456 | bytes 2883584 | tf_op jit(solution)/shard_map/dot_general | solution.py:24
  28.8 1.2 collective-permute-start.3
  29.9 0.5 divide_multiply_fusion.6
  30.5 0.5 divide_multiply_fusion.5
  31.0 0.5 multiply_convert_fusion.5
  31.5 2.4 %collective-permute-start.12 = (bf16[128,1024]{1,0:T(8,128)(2,1)S(1)}, bf16[128,1024]{1,0:T(8,128)(2,1)S(1)}, u32[]{:S(2)}, u32[]{:S(2)}) collective-permute-start(bf16[128,1024]{1,0:T(8,128)(2,1)S(1)} %multiply_convert_fusion.5), channel_id=1, source_target_pairs={{0,128},{16,144},{32,160},{48,176},{64,192},{80,208},{96,224},{112... | collective-permute-start | bytes 786440 | tf_op jit(solution)/shard_map/ppermute | solution.py:20
  34.4 1.7 %collective-permute-done.13 = bf16[128,1024]{1,0:T(8,128)(2,1)S(1)} collective-permute-done((bf16[128,1024]{1,0:T(8,128)(2,1)S(1)}, bf16[128,1024]{1,0:T(8,128)(2,1)S(1)}, u32[]{:S(2)}, u32[]{:S(2)}) %collective-permute-start.13) | collective-permute-done | bytes 262176 | tf_op jit(solution)/shard_map/ppermute | solution.py:20
  36.1 0.5 multiply_convert_fusion.4
  37.1 2.7 %collective-permute-start.14 = (bf16[128,1024]{1,0:T(8,128)(2,1)S(1)}, bf16[128,1024]{1,0:T(8,128)(2,1)S(1)}, u32[]{:S(2)}, u32[]{:S(2)}) collective-permute-start(bf16[128,1024]{1,0:T(8,128)(2,1)S(1)} %multiply_convert_fusion.4), channel_id=1, source_target_pairs={{0,128},{16,144},{32,160},{48,176},{64,192},{80,208},{96,224},{112... | collective-permute-start | bytes 786440 | tf_op jit(solution)/shard_map/ppermute | solution.py:20
  39.8 1.3 collective-permute-start.15
  41.8 1.7 %collective-permute-start.4 = (f32[128,256]{1,0:T(8,128)S(1)}, f32[128,256]{1,0:T(8,128)S(1)}, u32[]{:S(2)}, u32[]{:S(2)}) collective-permute-start(f32[128,256]{1,0:T(8,128)S(1)} %constant_dynamic-slice_fusion.4), channel_id=1, source_target_pairs={{0,64},{16,80},{32,96},{48,112},{64,0},{80,16},{96,32},{112,48},{1... | collective-permute-start | bytes 393224 | tf_op jit(solution)/shard_map/ppermute | solution.py:20
  44.0 1.8 %collective-permute-start.17 = (bf16[128,1024]{1,0:T(8,128)(2,1)S(1)}, bf16[128,1024]{1,0:T(8,128)(2,1)S(1)}, u32[]{:S(2)}, u32[]{:S(2)}) collective-permute-start(bf16[128,1024]{1,0:T(8,128)(2,1)S(1)} %slice.44), channel_id=1, source_target_pairs={{0,16},{16,0},{32,48},{48,32},{64,80},{80,64},{96,112},{112,96},{1... | collective-permute-start | bytes 786440 | tf_op jit(solution)/shard_map/ppermute | solution.py:20
  45.8 2.5 %collective-permute-done.4 = f32[128,256]{1,0:T(8,128)S(1)} collective-permute-done((f32[128,256]{1,0:T(8,128)S(1)}, f32[128,256]{1,0:T(8,128)S(1)}, u32[]{:S(2)}, u32[]{:S(2)}) %collective-permute-start.4) | collective-permute-done | bytes 131104 | tf_op jit(solution)/shard_map/ppermute | solution.py:20
  48.3 2.5 %collective-permute-start.5 = (bf16[128,256]{1,0:T(8,128)(2,1)S(1)}, bf16[128,256]{1,0:T(8,128)(2,1)S(1)}, u32[]{:S(2)}, u32[]{:S(2)}) collective-permute-start(bf16[128,256]{1,0:T(8,128)(2,1)S(1)} %convert_element_type.72), channel_id=1, source_target_pairs={{0,128},{16,144},{32,160},{48,176},{64,192},{80,208},{96,224},{112... | collective-permute-start | bytes 196616 | tf_op jit(solution)/shard_map/ppermute | solution.py:20
  50.7 0.5 multiply_convert_fusion.3
  51.4 0.5 multiply_convert_fusion.2
  51.9 3.8 %collective-permute-start.18 = (bf16[128,1024]{1,0:T(8,128)(2,1)S(1)}, bf16[128,1024]{1,0:T(8,128)(2,1)S(1)}, u32[]{:S(2)}, u32[]{:S(2)}) collective-permute-start(bf16[128,1024]{1,0:T(8,128)(2,1)S(1)} %multiply_convert_fusion.2), channel_id=1, source_target_pairs={{0,128},{16,144},{32,160},{48,176},{64,192},{80,208},{96,224},{112... | collective-permute-start | bytes 786440 | tf_op jit(solution)/shard_map/ppermute | solution.py:20
  55.7 0.5 divide_multiply_fusion.4
  56.2 0.5 fusion.18
  56.7 1.8 %collective-permute-done.14 = bf16[128,1024]{1,0:T(8,128)(2,1)S(1)} collective-permute-done((bf16[128,1024]{1,0:T(8,128)(2,1)S(1)}, bf16[128,1024]{1,0:T(8,128)(2,1)S(1)}, u32[]{:S(2)}, u32[]{:S(2)}) %collective-permute-start.14) | collective-permute-done | bytes 262176 | tf_op jit(solution)/shard_map/ppermute | solution.py:20
  58.5 0.5 divide_multiply_fusion.3
  59.0 0.5 fusion.16
  59.5 9.5 %collective-permute-done.5 = bf16[128,256]{1,0:T(8,128)(2,1)S(1)} collective-permute-done((bf16[128,256]{1,0:T(8,128)(2,1)S(1)}, bf16[128,256]{1,0:T(8,128)(2,1)S(1)}, u32[]{:S(2)}, u32[]{:S(2)}) %collective-permute-start.5) | collective-permute-done | bytes 65568 | tf_op jit(solution)/shard_map/ppermute | solution.py:20
  69.0 0.5 collective-permute-start.6
  70.0 14.5 %collective-permute-done.6 = bf16[128,256]{1,0:T(8,128)(2,1)S(1)} collective-permute-done((bf16[128,256]{1,0:T(8,128)(2,1)S(1)}, bf16[128,256]{1,0:T(8,128)(2,1)S(1)}, u32[]{:S(2)}, u32[]{:S(2)}) %collective-permute-start.6) | collective-permute-done | bytes 65568 | tf_op jit(solution)/shard_map/ppermute | solution.py:20
  84.6 1.0 collective-permute-start.7
  86.0 0.7 collective-permute-start.19
  86.7 0.9 collective-permute-start.21
  87.6 1.6 %collective-permute-done.7 = bf16[256,256]{1,0:T(8,128)(2,1)S(1)} collective-permute-done((bf16[256,256]{1,0:T(8,128)(2,1)S(1)}, bf16[256,256]{1,0:T(8,128)(2,1)S(1)}, u32[]{:S(2)}, u32[]{:S(2)}) %collective-permute-start.7) | collective-permute-done | bytes 131104 | tf_op jit(solution)/shard_map/ppermute | solution.py:20
  89.2 0.9 collective-permute-start.8
  90.2 0.5 divide_multiply_fusion.2
  90.7 0.5 divide_multiply_fusion.1
  91.2 5.0 %collective-permute-done.19 = bf16[160,1024]{1,0:T(8,128)(2,1)S(1)} collective-permute-done((bf16[160,1024]{1,0:T(8,128)(2,1)S(1)}, bf16[160,1024]{1,0:T(8,128)(2,1)S(1)}, u32[]{:S(2)}, u32[]{:S(2)}) %collective-permute-start.19) | collective-permute-done | bytes 327712 | tf_op jit(solution)/shard_map/ppermute | solution.py:20
  96.2 0.6 multiply_convert_fusion.1
  96.8 1.4 %collective-permute-start.20 = (bf16[160,1024]{1,0:T(8,128)(2,1)S(1)}, bf16[160,1024]{1,0:T(8,128)(2,1)S(1)}, u32[]{:S(2)}, u32[]{:S(2)}) collective-permute-start(bf16[160,1024]{1,0:T(8,128)(2,1)S(1)} %multiply_convert_fusion.1), channel_id=1, source_target_pairs={{0,128},{16,144},{32,160},{48,176},{64,192},{80,208},{96,224},{112... | collective-permute-start | bytes 983048 | tf_op jit(solution)/shard_map/ppermute | solution.py:20
  98.3 0.5 fusion.50
  98.8 4.5 %collective-permute-done.21 = bf16[160,1024]{1,0:T(8,128)(2,1)S(1)} collective-permute-done((bf16[160,1024]{1,0:T(8,128)(2,1)S(1)}, bf16[160,1024]{1,0:T(8,128)(2,1)S(1)}, u32[]{:S(2)}, u32[]{:S(2)}) %collective-permute-start.21) | collective-permute-done | bytes 327712 | tf_op jit(solution)/shard_map/ppermute | solution.py:20
  103.3 0.6 multiply_convert_fusion
  103.9 0.5 fusion.48
  104.4 1.2 collective-permute-start.22
  105.6 1.2 collective-permute-start.23
  107.3 2.5 %collective-permute-done.23 = bf16[64,1024]{1,0:T(8,128)(2,1)S(1)} collective-permute-done((bf16[64,1024]{1,0:T(8,128)(2,1)S(1)}, bf16[64,1024]{1,0:T(8,128)(2,1)S(1)}, u32[]{:S(2)}, u32[]{:S(2)}) %collective-permute-start.23) | collective-permute-done | bytes 131104 | tf_op jit(solution)/shard_map/ppermute | solution.py:20
  109.8 0.5 multiply_convert_fusion.6
  110.3 1.3 collective-permute-start.24
  115.0 18.7 %collective-permute-done.24 = bf16[64,1024]{1,0:T(8,128)(2,1)S(1)} collective-permute-done((bf16[64,1024]{1,0:T(8,128)(2,1)S(1)}, bf16[64,1024]{1,0:T(8,128)(2,1)S(1)}, u32[]{:S(2)}, u32[]{:S(2)}) %collective-permute-start.24) | collective-permute-done | bytes 131104 | tf_op jit(solution)/shard_map/ppermute | solution.py:20
  134.1 0.6 divide_multiply_fusion
  134.8 0.6 fusion.114
  135.5 1.3 copy-done.2
  136.8 0.7 fusion.165
  (78 shorter events, 7.8 us)
Async XLA Ops:
  0.0 112.2 %copy-start = (bf16[256,1024]{1,0:T(8,128)(2,1)S(1)}, bf16[256,1024]{1,0:T(8,128)(2,1)}, u32[]{:S(2)}) copy-start(bf16[256,1024]{1,0:T(8,128)(2,1)} %param.7) | copy-start | bytes 1572868
  1.6 10.6 %collective-permute-start = (bf16[64,1024]{1,0:T(8,128)(2,1)}, bf16[64,1024]{1,0:T(8,128)(2,1)}, u32[]{:S(2)}, u32[]{:S(2)}) collective-permute-start(bf16[64,1024]{1,0:T(8,128)(2,1)} %slice.36), channel_id=1, source_target_pairs={{0,16},{16,0},{32,48},{48,32},{64,80},{80,64},{96,112},{112,96},{1... | collective-permute-start | bytes 393224 | tf_op jit(solution)/shard_map/ppermute | solution.py:20
  6.1 1.1 copy-start.3
  7.2 21.5 %collective-permute-start.2 = (bf16[512,256]{1,0:T(8,128)(2,1)}, bf16[512,256]{1,0:T(8,128)(2,1)S(1)}, u32[]{:S(2)}, u32[]{:S(2)}) collective-permute-start(bf16[512,256]{1,0:T(8,128)(2,1)} %dynamic-slice_convert_fusion), channel_id=1, source_target_pairs={{0,48},{16,32},{32,16},{48,0},{64,112},{80,96},{96,80},{112,64},{1... | collective-permute-start | bytes 786440 | tf_op jit(solution)/shard_map/ppermute | solution.py:20
  11.7 7.2 %collective-permute-start.9 = (bf16[64,1024]{1,0:T(8,128)(2,1)S(1)}, bf16[64,1024]{1,0:T(8,128)(2,1)}, u32[]{:S(2)}, u32[]{:S(2)}) collective-permute-start(bf16[64,1024]{1,0:T(8,128)(2,1)S(1)} %get-tuple-element.27), channel_id=1, source_target_pairs={{0,16},{16,0},{32,48},{48,32},{64,80},{80,64},{96,112},{112,96},{1... | collective-permute-start | bytes 393224 | tf_op jit(solution)/shard_map/ppermute | solution.py:20
  13.6 16.3 %slice-start = ((s8[8388608]{0:T(1024)(128)(4,1)}), s8[4194304]{0:T(1024)(128)(4,1)S(1)}, s32[]{:S(2)}) async-start(s8[8388608]{0:T(1024)(128)(4,1)} %bitcast.172), calls=%async_computation | async-start | bytes 8388608
  15.8 14.1 %collective-permute-start.1 = (bf16[64,1024]{1,0:T(8,128)(2,1)S(1)}, bf16[64,1024]{1,0:T(8,128)(2,1)S(1)}, u32[]{:S(2)}, u32[]{:S(2)}) collective-permute-start(bf16[64,1024]{1,0:T(8,128)(2,1)S(1)} %multiply_convert_fusion.8), channel_id=1, source_target_pairs={{0,128},{16,144},{32,160},{48,176},{64,192},{80,208},{96,224},{112... | collective-permute-start | bytes 393224 | tf_op jit(solution)/shard_map/ppermute | solution.py:20
  18.9 3.8 %copy-start.1 = (bf16[1024,1024]{1,0:T(8,128)(2,1)S(1)}, bf16[1024,1024]{1,0:T(8,128)(2,1)}, u32[]{:S(2)}) copy-start(bf16[1024,1024]{1,0:T(8,128)(2,1)} %t_ref.1) | copy-start | bytes 6291460
  22.6 7.9 %collective-permute-start.10 = (bf16[64,1024]{1,0:T(8,128)(2,1)S(1)}, bf16[64,1024]{1,0:T(8,128)(2,1)S(1)}, u32[]{:S(2)}, u32[]{:S(2)}) collective-permute-start(bf16[64,1024]{1,0:T(8,128)(2,1)S(1)} %multiply_convert_fusion.7), channel_id=1, source_target_pairs={{0,128},{16,144},{32,160},{48,176},{64,192},{80,208},{96,224},{112... | collective-permute-start | bytes 393224 | tf_op jit(solution)/shard_map/ppermute | solution.py:20
  22.7 7.2 %slice-start.1 = ((s8[8388608]{0:T(1024)(128)(4,1)}), s8[4194304]{0:T(1024)(128)(4,1)S(1)}, s32[]{:S(2)}) async-start(s8[8388608]{0:T(1024)(128)(4,1)} %bitcast.172), calls=%async_computation.1 | async-start | bytes 8388608
  24.9 3.7 %copy-start.4 = (f32[1024,256]{1,0:T(8,128)S(1)}, f32[1024,256]{1,0:T(8,128)}, u32[]{:S(2)}) copy-start(f32[1024,256]{1,0:T(8,128)} %copy-done.3) | copy-start | bytes 3145732
  24.9 6.1 %collective-permute-start.11 = (bf16[128,1024]{1,0:T(8,128)(2,1)S(1)}, bf16[128,1024]{1,0:T(8,128)(2,1)S(1)}, u32[]{:S(2)}, u32[]{:S(2)}) collective-permute-start(bf16[128,1024]{1,0:T(8,128)(2,1)S(1)} %slice.39), channel_id=1, source_target_pairs={{0,16},{16,0},{32,48},{48,32},{64,80},{80,64},{96,112},{112,96},{1... | collective-permute-start | bytes 786440 | tf_op jit(solution)/shard_map/ppermute | solution.py:20
  26.1 10.0 %collective-permute-start.13 = (bf16[128,1024]{1,0:T(8,128)(2,1)S(1)}, bf16[128,1024]{1,0:T(8,128)(2,1)S(1)}, u32[]{:S(2)}, u32[]{:S(2)}) collective-permute-start(bf16[128,1024]{1,0:T(8,128)(2,1)S(1)} %slice.42), channel_id=1, source_target_pairs={{0,16},{16,0},{32,48},{48,32},{64,80},{80,64},{96,112},{112,96},{1... | collective-permute-start | bytes 786440 | tf_op jit(solution)/shard_map/ppermute | solution.py:20
  28.8 13.0 %collective-permute-start.3 = (f32[256,256]{1,0:T(8,128)S(1)}, f32[256,256]{1,0:T(8,128)S(1)}, u32[]{:S(2)}, u32[]{:S(2)}) collective-permute-start(f32[256,256]{1,0:T(8,128)S(1)} %constant_dynamic-slice_fusion.5), channel_id=1, source_target_pairs={{0,16},{16,0},{32,48},{48,32},{64,80},{80,64},{96,112},{112,96},{1... | collective-permute-start | bytes 786440 | tf_op jit(solution)/shard_map/ppermute | solution.py:20
  31.5 24.1 %collective-permute-start.12 = (bf16[128,1024]{1,0:T(8,128)(2,1)S(1)}, bf16[128,1024]{1,0:T(8,128)(2,1)S(1)}, u32[]{:S(2)}, u32[]{:S(2)}) collective-permute-start(bf16[128,1024]{1,0:T(8,128)(2,1)S(1)} %multiply_convert_fusion.5), channel_id=1, source_target_pairs={{0,128},{16,144},{32,160},{48,176},{64,192},{80,208},{96,224},{112... | collective-permute-start | bytes 786440 | tf_op jit(solution)/shard_map/ppermute | solution.py:20
  37.1 21.4 %collective-permute-start.14 = (bf16[128,1024]{1,0:T(8,128)(2,1)S(1)}, bf16[128,1024]{1,0:T(8,128)(2,1)S(1)}, u32[]{:S(2)}, u32[]{:S(2)}) collective-permute-start(bf16[128,1024]{1,0:T(8,128)(2,1)S(1)} %multiply_convert_fusion.4), channel_id=1, source_target_pairs={{0,128},{16,144},{32,160},{48,176},{64,192},{80,208},{96,224},{112... | collective-permute-start | bytes 786440 | tf_op jit(solution)/shard_map/ppermute | solution.py:20
  39.8 10.9 %collective-permute-start.15 = (bf16[128,1024]{1,0:T(8,128)(2,1)S(1)}, bf16[128,1024]{1,0:T(8,128)(2,1)S(1)}, u32[]{:S(2)}, u32[]{:S(2)}) collective-permute-start(bf16[128,1024]{1,0:T(8,128)(2,1)S(1)} %slice.43), channel_id=1, source_target_pairs={{0,16},{16,0},{32,48},{48,32},{64,80},{80,64},{96,112},{112,96},{1... | collective-permute-start | bytes 786440 | tf_op jit(solution)/shard_map/ppermute | solution.py:20
  41.8 6.4 %collective-permute-start.4 = (f32[128,256]{1,0:T(8,128)S(1)}, f32[128,256]{1,0:T(8,128)S(1)}, u32[]{:S(2)}, u32[]{:S(2)}) collective-permute-start(f32[128,256]{1,0:T(8,128)S(1)} %constant_dynamic-slice_fusion.4), channel_id=1, source_target_pairs={{0,64},{16,80},{32,96},{48,112},{64,0},{80,16},{96,32},{112,48},{1... | collective-permute-start | bytes 393224 | tf_op jit(solution)/shard_map/ppermute | solution.py:20
  44.0 7.4 %collective-permute-start.17 = (bf16[128,1024]{1,0:T(8,128)(2,1)S(1)}, bf16[128,1024]{1,0:T(8,128)(2,1)S(1)}, u32[]{:S(2)}, u32[]{:S(2)}) collective-permute-start(bf16[128,1024]{1,0:T(8,128)(2,1)S(1)} %slice.44), channel_id=1, source_target_pairs={{0,16},{16,0},{32,48},{48,32},{64,80},{80,64},{96,112},{112,96},{1... | collective-permute-start | bytes 786440 | tf_op jit(solution)/shard_map/ppermute | solution.py:20
  48.3 20.7 %collective-permute-start.5 = (bf16[128,256]{1,0:T(8,128)(2,1)S(1)}, bf16[128,256]{1,0:T(8,128)(2,1)S(1)}, u32[]{:S(2)}, u32[]{:S(2)}) collective-permute-start(bf16[128,256]{1,0:T(8,128)(2,1)S(1)} %convert_element_type.72), channel_id=1, source_target_pairs={{0,128},{16,144},{32,160},{48,176},{64,192},{80,208},{96,224},{112... | collective-permute-start | bytes 196616 | tf_op jit(solution)/shard_map/ppermute | solution.py:20
  51.3 38.9 %collective-permute-start.16 = (bf16[128,1024]{1,0:T(8,128)(2,1)S(1)}, bf16[128,1024]{1,0:T(8,128)(2,1)S(1)}, u32[]{:S(2)}, u32[]{:S(2)}) collective-permute-start(bf16[128,1024]{1,0:T(8,128)(2,1)S(1)} %multiply_convert_fusion.3), channel_id=1, source_target_pairs={{0,128},{16,144},{32,160},{48,176},{64,192},{80,208},{96,224},{112... | collective-permute-start | bytes 786440 | tf_op jit(solution)/shard_map/ppermute | solution.py:20
  51.9 38.8 %collective-permute-start.18 = (bf16[128,1024]{1,0:T(8,128)(2,1)S(1)}, bf16[128,1024]{1,0:T(8,128)(2,1)S(1)}, u32[]{:S(2)}, u32[]{:S(2)}) collective-permute-start(bf16[128,1024]{1,0:T(8,128)(2,1)S(1)} %multiply_convert_fusion.2), channel_id=1, source_target_pairs={{0,128},{16,144},{32,160},{48,176},{64,192},{80,208},{96,224},{112... | collective-permute-start | bytes 786440 | tf_op jit(solution)/shard_map/ppermute | solution.py:20
  69.0 15.5 %collective-permute-start.6 = (bf16[128,256]{1,0:T(8,128)(2,1)S(1)}, bf16[128,256]{1,0:T(8,128)(2,1)S(1)}, u32[]{:S(2)}, u32[]{:S(2)}) collective-permute-start(bf16[128,256]{1,0:T(8,128)(2,1)S(1)} %add_convert_fusion.9), channel_id=1, source_target_pairs={{0,64},{16,80},{32,96},{48,112},{64,0},{80,16},{96,32},{112,48},{1... | collective-permute-start | bytes 196616 | tf_op jit(solution)/shard_map/ppermute | solution.py:20
  84.6 4.7 %collective-permute-start.7 = (bf16[256,256]{1,0:T(8,128)(2,1)S(1)}, bf16[256,256]{1,0:T(8,128)(2,1)S(1)}, u32[]{:S(2)}, u32[]{:S(2)}) collective-permute-start(bf16[256,256]{1,0:T(8,128)(2,1)S(1)} %pad_maximum_fusion.2), channel_id=1, source_target_pairs={{0,16},{16,0},{32,48},{48,32},{64,80},{80,64},{96,112},{112,96},{1... | collective-permute-start | bytes 393224 | tf_op jit(solution)/shard_map/ppermute | solution.py:20
  86.0 10.2 %collective-permute-start.19 = (bf16[160,1024]{1,0:T(8,128)(2,1)S(1)}, bf16[160,1024]{1,0:T(8,128)(2,1)S(1)}, u32[]{:S(2)}, u32[]{:S(2)}) collective-permute-start(bf16[160,1024]{1,0:T(8,128)(2,1)S(1)} %slice.45), channel_id=1, source_target_pairs={{0,16},{16,0},{32,48},{48,32},{64,80},{80,64},{96,112},{112,96},{1... | collective-permute-start | bytes 983048 | tf_op jit(solution)/shard_map/ppermute | solution.py:20
  86.7 16.5 %collective-permute-start.21 = (bf16[160,1024]{1,0:T(8,128)(2,1)S(1)}, bf16[160,1024]{1,0:T(8,128)(2,1)S(1)}, u32[]{:S(2)}, u32[]{:S(2)}) collective-permute-start(bf16[160,1024]{1,0:T(8,128)(2,1)S(1)} %slice.46), channel_id=1, source_target_pairs={{0,16},{16,0},{32,48},{48,32},{64,80},{80,64},{96,112},{112,96},{1... | collective-permute-start | bytes 983048 | tf_op jit(solution)/shard_map/ppermute | solution.py:20
  89.2 22.9 %collective-permute-start.8 = (bf16[512,256]{1,0:T(8,128)(2,1)S(1)}, bf16[512,256]{1,0:T(8,128)(2,1)S(1)}, u32[]{:S(2)}, u32[]{:S(2)}) collective-permute-start(bf16[512,256]{1,0:T(8,128)(2,1)S(1)} %pad_maximum_fusion.1), channel_id=1, source_target_pairs={{0,48},{16,32},{32,16},{48,0},{64,112},{80,96},{96,80},{112,64},{1... | collective-permute-start | bytes 786440 | tf_op jit(solution)/shard_map/ppermute | solution.py:20
  96.8 37.3 %collective-permute-start.20 = (bf16[160,1024]{1,0:T(8,128)(2,1)S(1)}, bf16[160,1024]{1,0:T(8,128)(2,1)S(1)}, u32[]{:S(2)}, u32[]{:S(2)}) collective-permute-start(bf16[160,1024]{1,0:T(8,128)(2,1)S(1)} %multiply_convert_fusion.1), channel_id=1, source_target_pairs={{0,128},{16,144},{32,160},{48,176},{64,192},{80,208},{96,224},{112... | collective-permute-start | bytes 983048 | tf_op jit(solution)/shard_map/ppermute | solution.py:20
  104.4 30.5 %collective-permute-start.22 = (bf16[160,1024]{1,0:T(8,128)(2,1)S(1)}, bf16[160,1024]{1,0:T(8,128)(2,1)S(1)}, u32[]{:S(2)}, u32[]{:S(2)}) collective-permute-start(bf16[160,1024]{1,0:T(8,128)(2,1)S(1)} %multiply_convert_fusion), channel_id=1, source_target_pairs={{0,128},{16,144},{32,160},{48,176},{64,192},{80,208},{96,224},{112... | collective-permute-start | bytes 983048 | tf_op jit(solution)/shard_map/ppermute | solution.py:20
  105.6 4.2 %collective-permute-start.23 = (bf16[64,1024]{1,0:T(8,128)(2,1)S(1)}, bf16[64,1024]{1,0:T(8,128)(2,1)S(1)}, u32[]{:S(2)}, u32[]{:S(2)}) collective-permute-start(bf16[64,1024]{1,0:T(8,128)(2,1)S(1)} %slice.47), channel_id=1, source_target_pairs={{0,16},{16,0},{32,48},{48,32},{64,80},{80,64},{96,112},{112,96},{1... | collective-permute-start | bytes 393224 | tf_op jit(solution)/shard_map/ppermute | solution.py:20
  110.3 23.3 %collective-permute-start.24 = (bf16[64,1024]{1,0:T(8,128)(2,1)S(1)}, bf16[64,1024]{1,0:T(8,128)(2,1)S(1)}, u32[]{:S(2)}, u32[]{:S(2)}) collective-permute-start(bf16[64,1024]{1,0:T(8,128)(2,1)S(1)} %multiply_convert_fusion.6), channel_id=1, source_target_pairs={{0,128},{16,144},{32,160},{48,176},{64,192},{80,208},{96,224},{112... | collective-permute-start | bytes 393224 | tf_op jit(solution)/shard_map/ppermute | solution.py:20
  135.5 1.3 copy-start.2
